TPU v7x, 512 devices: a whole 4x4x16 slice. The times are simulated.
512 devices in a mesh: dp: 16 (over x, y), mp: 32 (over z, core).
Axes of the slice: x: 4, y: 4, z: 16, core: 2. Of those that a mesh axis runs over, the one named last changes fastest.
Arguments:
- hidden_policy: bfloat16 [256, 16, 2048], P('dp', None, 'mp'), may hold values from -6 to 6
- hidden_reference: bfloat16 [256, 16, 2048], P('dp', None, 'mp'), may hold values from -6 to 6
- ffn_gain_policy: float32 [2048], replicated, may hold values from 0.1 to 1.9
- ffn_gain_reference: float32 [2048], replicated, may hold values from 0.1 to 1.9
- up_policy: bfloat16 [2048, 4096], P(None, 'mp'), may hold values from -0.125 to 0.125
- up_reference: bfloat16 [2048, 4096], P(None, 'mp'), may hold values from -0.125 to 0.125
- down_policy: bfloat16 [4096, 2048], P('mp'), may hold values from -0.1875 to 0.1875
- down_reference: bfloat16 [4096, 2048], P('mp'), may hold values from -0.1875 to 0.1875
- final_gain_policy: float32 [2048], replicated, may hold values from 0.1 to 1.9
- final_gain_reference: float32 [2048], replicated, may hold values from 0.1 to 1.9
- out_policy: bfloat16 [2048, 28672], P('dp', 'mp'), may hold values from -4 to 4
- out_reference: bfloat16 [2048, 28672], P('dp', 'mp'), may hold values from -4 to 4
- move_plan: int32 [256], replicated, may hold values from 0 to 255, as said below
- lengths: int32 [256], P('dp'), may hold values from 1 to 16, 2048 in all
- targets: int32 [256, 16], P('dp'), may hold values from 0 to 28671
Outputs:
- token_diff: float32 [256, 16], P('dp')
- seq_diff: float32 [256], P('dp')
Inputs may be any that keep to these rules, and one draw needn't show every extreme that they name: `move_plan`: A permutation of the slots; slot // 16 is the owning index of dp, each owning exactly 16 requests; from one index of dp to one owner go either no requests or exactly 2.
All inputs are finite; a program needn't handle non-finite values. No bound on the sum of `lengths` on one device may be relied on, other than what follows from the above.
Results may differ from a plain program's by a relative error of at most 0.0081.
Values may be sent and summed in bfloat16 or wider, within the bound.
A program may use at most 64 MiB of HBM per device.

v0:
```python
import jax
import jax.numpy as jnp
from jax import lax
from jax.sharding import PartitionSpec as P

D = 2048


epsilon = 1e-05


def select_rows(selector, values):
    return jnp.dot(selector, values, preferred_element_type=jnp.float32).astype(jnp.bfloat16)


def norm_from_sums(values, first_sum, second_sum, gain, width):
    center = first_sum / width
    spread = second_sum / width - center * center
    return (values - center[:, None]) * lax.rsqrt(spread + epsilon)[:, None] * gain


def local(
    hidden_policy,
    hidden_reference,
    ffn_gain_policy,
    ffn_gain_reference,
    up_policy,
    up_reference,
    down_policy,
    down_reference,
    final_gain_policy,
    final_gain_reference,
    out_policy,
    out_reference,
    move_plan,
    lengths,
    targets,
):
    dp_count = lax.axis_size("dp")
    dp_index = lax.axis_index("dp")
    mp_index = lax.axis_index("mp")
    req_count = hidden_policy.shape[0]
    slot_count = hidden_policy.shape[1]
    width_part = hidden_policy.shape[2]
    tokens_here = req_count * slot_count
    capacity = max(2, req_count // min(8, dp_count))
    buffer_slots = dp_count * capacity
    plan = move_plan.reshape(dp_count, req_count)
    owner_device = plan // req_count
    positions = jnp.arange(req_count, dtype=jnp.int32)
    earlier = positions[None, :] < positions[:, None]
    same_owner = owner_device[:, :, None] == owner_device[:, None, :]
    rank = jnp.sum(jnp.logical_and(same_owner, earlier[None]), axis=2)
    own_owner = lax.dynamic_index_in_dim(owner_device, dp_index, 0, keepdims=False)
    own_rank = lax.dynamic_index_in_dim(rank, dp_index, 0, keepdims=False)
    send_slot = own_owner * capacity + own_rank
    send_select = (jnp.arange(buffer_slots, dtype=jnp.int32)[:, None] == send_slot[None, :]).astype(
        jnp.bfloat16
    )
    packed = (
        select_rows(send_select, hidden_policy.reshape(req_count, slot_count * width_part)),
        select_rows(send_select, hidden_reference.reshape(req_count, slot_count * width_part)),
    )
    arrived = (
        lax.all_to_all(packed[0], "dp", split_axis=0, concat_axis=0, tiled=True),
        lax.all_to_all(packed[1], "dp", split_axis=0, concat_axis=0, tiled=True),
    )
    column = jnp.arange(dp_count, dtype=jnp.int32)[:, None] * capacity + rank
    local_row = plan - dp_index * req_count
    owned = owner_device == dp_index
    row_hot = jnp.logical_and(
        local_row.reshape(-1)[:, None] == positions[None, :], owned.reshape(-1)[:, None]
    ).astype(jnp.bfloat16)
    column_hot = (
        column.reshape(-1)[:, None] == jnp.arange(buffer_slots, dtype=jnp.int32)[None, :]
    ).astype(jnp.bfloat16)
    receive_select = jnp.dot(row_hot.T, column_hot, preferred_element_type=jnp.float32).astype(
        jnp.bfloat16
    )
    moved_policy = select_rows(receive_select, arrived[0]).reshape(tokens_here, width_part)
    moved_reference = select_rows(receive_select, arrived[1]).reshape(tokens_here, width_part)
    stream_policy = moved_policy.astype(jnp.float32)
    stream_reference = moved_reference.astype(jnp.float32)
    ffn_sums = lax.psum(
        (
            jnp.sum(stream_policy, axis=1),
            jnp.sum(stream_policy * stream_policy, axis=1),
            jnp.sum(stream_reference, axis=1),
            jnp.sum(stream_reference * stream_reference, axis=1),
        ),
        "mp",
    )
    gain_policy_part = lax.dynamic_slice_in_dim(ffn_gain_policy, mp_index * width_part, width_part)
    gain_reference_part = lax.dynamic_slice_in_dim(
        ffn_gain_reference, mp_index * width_part, width_part
    )
    normed_policy = norm_from_sums(
        stream_policy, ffn_sums[0], ffn_sums[1], gain_policy_part, D
    ).astype(jnp.bfloat16)
    normed_reference = norm_from_sums(
        stream_reference, ffn_sums[2], ffn_sums[3], gain_reference_part, D
    ).astype(jnp.bfloat16)
    pieces = (
        lax.all_gather(normed_policy, "mp", axis=1, tiled=True),
        lax.all_gather(normed_reference, "mp", axis=1, tiled=True),
    )
    pre_policy = jnp.dot(pieces[0], up_policy, preferred_element_type=jnp.float32)
    pre_reference = jnp.dot(pieces[1], up_reference, preferred_element_type=jnp.float32)
    units_policy = jax.nn.gelu(pre_policy).astype(jnp.bfloat16)
    units_reference = jax.nn.gelu(pre_reference).astype(jnp.bfloat16)
    terms = (
        jnp.dot(units_policy, down_policy, preferred_element_type=jnp.float32),
        jnp.dot(units_reference, down_reference, preferred_element_type=jnp.float32),
    )
    summed = (
        lax.psum_scatter(terms[0], "mp", scatter_dimension=1, tiled=True),
        lax.psum_scatter(terms[1], "mp", scatter_dimension=1, tiled=True),
    )
    after_policy = stream_policy + summed[0]
    after_reference = stream_reference + summed[1]
    final_sums = lax.psum(
        (
            jnp.sum(after_policy, axis=1),
            jnp.sum(after_policy * after_policy, axis=1),
            jnp.sum(after_reference, axis=1),
            jnp.sum(after_reference * after_reference, axis=1),
        ),
        "mp",
    )
    final_policy_part = lax.dynamic_slice_in_dim(
        final_gain_policy, mp_index * width_part, width_part
    )
    final_reference_part = lax.dynamic_slice_in_dim(
        final_gain_reference, mp_index * width_part, width_part
    )
    out_normed_policy = norm_from_sums(
        after_policy, final_sums[0], final_sums[1], final_policy_part, D
    ).astype(jnp.bfloat16)
    out_normed_reference = norm_from_sums(
        after_reference, final_sums[2], final_sums[3], final_reference_part, D
    ).astype(jnp.bfloat16)
    full_policy, full_reference = (
        lax.all_gather(out_normed_policy, "mp", axis=1, tiled=True),
        lax.all_gather(out_normed_reference, "mp", axis=1, tiled=True),
    )
    vocab_part = out_policy.shape[1]
    pieces = (
        lax.all_gather(out_policy, "dp", axis=0, tiled=True),
        lax.all_gather(out_reference, "dp", axis=0, tiled=True),
    )
    logits_policy = jnp.dot(full_policy, pieces[0], preferred_element_type=jnp.float32)
    logits_reference = jnp.dot(full_reference, pieces[1], preferred_element_type=jnp.float32)
    wanted = targets.reshape(tokens_here)
    entry_ids = jnp.arange(vocab_part, dtype=jnp.int32)[None, :] + mp_index * vocab_part
    target_hit = entry_ids == wanted[:, None]
    picked_policy = jnp.sum(jnp.where(target_hit, logits_policy, 0.0), axis=1)
    picked_reference = jnp.sum(jnp.where(target_hit, logits_reference, 0.0), axis=1)
    top_policy, top_reference = lax.pmax(
        (jnp.max(logits_policy, axis=1), jnp.max(logits_reference, axis=1)), "mp"
    )
    totals = lax.psum(
        (
            jnp.sum(jnp.exp(logits_policy - top_policy[:, None]), axis=1),
            jnp.sum(jnp.exp(logits_reference - top_reference[:, None]), axis=1),
            picked_policy,
            picked_reference,
        ),
        "mp",
    )
    logprob_policy = totals[2] - (top_policy + jnp.log(totals[0]))
    logprob_reference = totals[3] - (top_reference + jnp.log(totals[1]))
    live = jnp.arange(slot_count, dtype=jnp.int32)[None, :] < lengths[:, None]
    token_diff = jnp.where(
        live, (logprob_policy - logprob_reference).reshape(req_count, slot_count), jnp.float32(0.0)
    )
    seq_diff = jnp.sum(token_diff, axis=1)
    return (token_diff, seq_diff)


def solution(mesh):
    return jax.shard_map(
        local,
        mesh=mesh,
        in_specs=(
            P("dp", None, "mp"),
            P("dp", None, "mp"),
            P(),
            P(),
            P(None, "mp"),
            P(None, "mp"),
            P("mp", None),
            P("mp", None),
            P(),
            P(),
            P("dp", "mp"),
            P("dp", "mp"),
            P(),
            P("dp"),
            P("dp", None),
        ),
        out_specs=(P("dp", None), P("dp")),
        check_vma=False,
    )
```

profile of v0, /device:TPU:1, one launch (start us, length us, event | category | flops | bytes accessed | tf_op | source)
XLA Modules:
  0.0 811.6 jit_solution(14091598724623640920)
XLA Ops:
  8.0 0.8 reshape.153
  8.9 1.0 reshape.155
  11.1 7.6 all-to-all-start.1
  18.6 0.7 fusion.42
  20.2 1.0 reshape.154
  22.2 0.8 dynamic_slice.23
  23.0 2.2 all-to-all-done.1
  25.2 4.5 all-to-all-start
  30.0 6.2 all-to-all-done
  36.8 54.5 %all-reduce.2 = (f32[256]{0:T(256)S(1)}, f32[256]{0:T(256)S(1)}, f32[256]{0:T(256)S(1)}, f32[256]{0:T(256)S(1)}) all-reduce(f32[256]{0:T(256)S(1)} %get-tuple-element.46, f32[256]{0:T(256)S(1)} %get-tuple-element.47, f32[256]{0:T(256)S(1)} %get-tuple-element.7, f32[256]{0:T(256)S(1)} %get-tuple-element.6), channel_id=1, replica_groups=mesh['dp'=16,'mp'=32] {'mp'}, use_global_device_ids=true, to_apply=%region_19.20 | all-reduce | flops 1024 | bytes 8192 | tf_op jit(solution)/shard_map/psum | solution.py:84
  91.2 0.7 multiply_convert_fusion.1
  92.0 0.8 dynamic_slice.21
  93.6 63.8 %all-gather.13.cloned.1.call-done = bf16[256,2048]{0,1:T(8,128)(2,1)} async-done(((bf16[256,64]{0,1:T(8,128)(2,1)}), bf16[256,2048]{0,1:T(8,128)(2,1)}) %all-gather.13.cloned.1.call-update) | async-done | bytes 1048592 | tf_op jit(solution)/shard_map/all_gather | solution.py:105
  157.4 3.6 fusion.22
  161.1 66.3 %all-gather.7.cloned.1.call-done = bf16[256,2048]{0,1:T(8,128)(2,1)} async-done(((bf16[256,64]{0,1:T(8,128)(2,1)}), bf16[256,2048]{0,1:T(8,128)(2,1)}) %all-gather.7.cloned.1.call-update) | async-done | bytes 1048592 | tf_op jit(solution)/shard_map/all_gather | solution.py:104
  227.4 3.4 fusion.24
  231.5 0.8 dynamic_slice.24
  232.2 102.6 %reduce-scatter.5.cloned.1.call-done = f32[256,64]{0,1:T(8,128)} async-done(((f32[256,2048]{0,1:T(8,128)}), f32[256,64]{0,1:T(8,128)}) %reduce-scatter.5.cloned.1.call-update) | async-done | bytes 65552 | tf_op jit(solution)/shard_map/reduce_scatter | solution.py:117
  334.9 0.9 fusion.54
  335.7 109.6 %reduce-scatter.3.cloned.1.call-done = f32[256,64]{0,1:T(8,128)} async-done(((f32[256,2048]{0,1:T(8,128)}), f32[256,64]{0,1:T(8,128)}) %reduce-scatter.3.cloned.1.call-update) | async-done | bytes 65552 | tf_op jit(solution)/shard_map/reduce_scatter | solution.py:116
  445.4 0.9 fusion.53
  446.2 48.8 %all-reduce.1 = (f32[256]{0:T(256)S(1)}, f32[256]{0:T(256)S(1)}, f32[256]{0:T(256)S(1)}, f32[256]{0:T(256)S(1)}) all-reduce(f32[256]{0:T(256)S(1)} %get-tuple-element.13, f32[256]{0:T(256)S(1)} %get-tuple-element.12, f32[256]{0:T(256)S(1)} %get-tuple-element.11, f32[256]{0:T(256)S(1)} %get-tuple-element.10), channel_id=1, replica_groups=mesh['dp'=16,'mp'=32] {'mp'}, use_global_device_ids=true, to_apply=%region_24.25 | all-reduce | flops 1024 | bytes 8192 | tf_op jit(solution)/shard_map/psum | solution.py:121
  495.0 0.7 multiply_convert_fusion
  496.4 0.8 dynamic_slice.22
  498.0 69.6 %all-gather.15.cloned.1.call-done = bf16[256,2048]{0,1:T(8,128)(2,1)} async-done(((bf16[256,64]{0,1:T(8,128)(2,1)}), bf16[256,2048]{0,1:T(8,128)(2,1)}) %all-gather.15.cloned.1.call-update) | async-done | bytes 1048592 | tf_op jit(solution)/shard_map/all_gather | solution.py:144
  567.6 3.7 fusion.57
  571.3 60.5 %all-gather.11.cloned.1.call-done = bf16[2048,896]{1,0:T(8,128)(2,1)} async-done(((bf16[128,896]{1,0:T(8,128)(2,1)}), bf16[2048,896]{1,0:T(8,128)(2,1)}) %all-gather.11.cloned.1.call-update) | async-done | bytes 3670032 | tf_op jit(solution)/shard_map/all_gather | solution.py:148
  631.8 73.1 %all-gather.9.cloned.1.call-done = bf16[256,2048]{0,1:T(8,128)(2,1)} async-done(((bf16[256,64]{0,1:T(8,128)(2,1)}), bf16[256,2048]{0,1:T(8,128)(2,1)}) %all-gather.9.cloned.1.call-update) | async-done | bytes 1048592 | tf_op jit(solution)/shard_map/all_gather | solution.py:143
  704.9 3.7 fusion.58
  708.6 45.4 %all-reduce.3 = (f32[256]{0:T(256)S(1)}, f32[256]{0:T(256)S(1)}) all-reduce(f32[256]{0:T(256)S(1)} %get-tuple-element.42, f32[256]{0:T(256)S(1)} %get-tuple-element.44), channel_id=1, replica_groups=mesh['dp'=16,'mp'=32] {'mp'}, use_global_device_ids=true, to_apply=%region_28.29 | all-reduce | flops 512 | bytes 4096 | tf_op jit(solution)/shard_map/pmax | solution.py:158
  754.6 48.2 %all-reduce = (f32[256]{0:T(256)S(1)}, f32[256]{0:T(256)S(1)}, f32[256]{0:T(256)S(1)}, f32[256]{0:T(256)S(1)}) all-reduce(f32[256]{0:T(256)S(1)} %get-tuple-element.32, f32[256]{0:T(256)S(1)} %get-tuple-element.33, f32[256]{0:T(256)S(1)} %get-tuple-element.3, f32[256]{0:T(256)S(1)} %get-tuple-element.2), channel_id=1, replica_groups=mesh['dp'=16,'mp'=32] {'mp'}, use_global_device_ids=true, to_apply=%region_26.27 | all-reduce | flops 1024 | bytes 8192 | tf_op jit(solution)/shard_map/psum | solution.py:161
  802.9 1.3 fusion.55
  (60 shorter events, 7.8 us)
Async XLA Ops:
  8.0 149.4 %copy-start = (bf16[128,2048]{1,0:T(8,128)(2,1)S(1)}, bf16[128,2048]{1,0:T(8,128)(2,1)}, u32[]{:S(2)}) copy-start(bf16[128,2048]{1,0:T(8,128)(2,1)} %param.22) | copy-start | bytes 1572868
  11.1 14.1 %all-to-all-start.1 = ((bf16[16,2,1024]{2,1,0:T(2,128)(2,1)}), bf16[16,2,1024]{2,1,0:T(2,128)(2,1)S(1)}, u32[]{:S(2)}, u32[]{:S(2)}) async-start(bf16[16,2,1024]{2,1,0:T(2,128)(2,1)} %all_to_all.19), calls=%async_computation.2 | async-start | bytes 131072 | tf_op jit(solution)/shard_map/all_to_all | solution.py:66
  25.2 11.0 %all-to-all-start = ((bf16[16,2,1024]{2,1,0:T(2,128)(2,1)}), bf16[16,2,1024]{2,1,0:T(2,128)(2,1)S(1)}, u32[]{:S(2)}, u32[]{:S(2)}) async-start(bf16[16,2,1024]{2,1,0:T(2,128)(2,1)} %all_to_all.16), calls=%async_computation | async-start | bytes 131072 | tf_op jit(solution)/shard_map/all_to_all | solution.py:65
  29.7 127.7 %all-gather.13.cloned.1.call-start = ((), (), s32[]{:S(2)}) async-start(), calls=%async_computation.8 | async-start | bytes 1081344 | tf_op jit(solution)/shard_map/all_gather | solution.py:105
  36.4 190.9 %copy-start.1 = (bf16[128,2048]{1,0:T(8,128)(2,1)S(1)}, bf16[128,2048]{1,0:T(8,128)(2,1)}, u32[]{:S(2)}) copy-start(bf16[128,2048]{1,0:T(8,128)(2,1)} %param.21) | copy-start | bytes 1572868
  36.4 190.9 %copy-start.2 = (bf16[2048,128]{1,0:T(8,128)(2,1)S(1)}, bf16[2048,128]{1,0:T(8,128)(2,1)}, u32[]{:S(2)}) copy-start(bf16[2048,128]{1,0:T(8,128)(2,1)} %param.19) | copy-start | bytes 1572868
  92.0 135.4 %all-gather.7.cloned.1.call-start = ((), (), s32[]{:S(2)}) async-start(), calls=%async_computation.4 | async-start | bytes 1081344 | tf_op jit(solution)/shard_map/all_gather | solution.py:104
  93.6 241.3 %reduce-scatter.5.cloned.1.call-start = ((), (), s32[]{:S(2)}) async-start(), calls=%async_computation.9 | async-start | bytes 2162688 | tf_op jit(solution)/shard_map/reduce_scatter | solution.py:117
  161.0 336.8 %copy-start.3 = (s32[16,16]{1,0:T(8,128)S(1)}, s32[16,16]{1,0:T(8,128)}, u32[]{:S(2)}) copy-start(s32[16,16]{1,0:T(8,128)} %param.29) | copy-start | bytes 3076
  161.0 284.3 %reduce-scatter.3.cloned.1.call-start = ((), (), s32[]{:S(2)}) async-start(), calls=%async_computation.5 | async-start | bytes 2162688 | tf_op jit(solution)/shard_map/reduce_scatter | solution.py:116
  230.8 267.1 %all-gather.17.cloned.1.call-start = ((), (), s32[]{:S(2)}) async-start(), calls=%async_computation.11 | async-start | bytes 3899392 | tf_op jit(solution)/shard_map/all_gather | solution.py:149
  231.4 336.2 %all-gather.15.cloned.1.call-start = ((), (), s32[]{:S(2)}) async-start(), calls=%async_computation.10 | async-start | bytes 1081344 | tf_op jit(solution)/shard_map/all_gather | solution.py:144
  495.7 136.1 %all-gather.11.cloned.1.call-start = ((), (), s32[]{:S(2)}) async-start(), calls=%async_computation.7 | async-start | bytes 3899392 | tf_op jit(solution)/shard_map/all_gather | solution.py:148
  496.3 208.6 %all-gather.9.cloned.1.call-start = ((), (), s32[]{:S(2)}) async-start(), calls=%async_computation.6 | async-start | bytes 1081344 | tf_op jit(solution)/shard_map/all_gather | solution.py:143
  571.3 231.6 %copy-start.4 = (s32[16]{0:T(128)S(1)}, s32[16]{0:T(128)}, u32[]{:S(2)}) copy-start(s32[16]{0:T(128)} %param.28) | copy-start | bytes 196
Sparse Core Ops, SparseCore 0:
  92.1 65.2 all-gather.12
  159.5 67.8 all-gather.6
  230.2 104.6 reduce-scatter.4
  337.8 107.5 reduce-scatter.2
Sparse Core Ops, SparseCore 1:
  234.4 61.3 all-gather.16
  495.8 71.7 all-gather.14
  570.5 61.2 all-gather.10
  633.9 70.9 all-gather.8
where the time goes:
time: 812 us
  waiting for transfers between devices  555 us (68%)
  blocking collectives  197 us (24%)
  between operations  15.6 us (2%)
  matrix products  15.3 us (2%)
  starting transfers between devices  12.4 us (2%)
  other arithmetic  8.56 us (1%)
    reduce_scatter x1, waiting for transfers between devices, local(): lax.psum_scatter(terms[0], 'mp', scatter_dimension=1, tiled=True)  110 us
    reduce_scatter x1, waiting for transfers between devices, local(): lax.psum_scatter(terms[1], 'mp', scatter_dimension=1, tiled=True)  103 us
    all_gather x1, waiting for transfers between devices, local(): lax.all_gather(out_normed_policy, 'mp', axis=1, tiled=True)  73.1 us
    all_gather x1, waiting for transfers between devices, local(): lax.all_gather(out_normed_reference, 'mp', axis=1, tiled=True)  69.6 us
    all_gather x1, waiting for transfers between devices, local(): lax.all_gather(normed_policy, 'mp', axis=1, tiled=True)  66.3 us
    all_gather x1, waiting for transfers between devices, local(): lax.all_gather(normed_reference, 'mp', axis=1, tiled=True)  63.8 us
    all_gather x1, waiting for transfers between devices, local(): lax.all_gather(out_policy, 'dp', axis=0, tiled=True)  60.5 us
    psum x1, blocking collectives, local(): lax.psum((jnp.sum(stream_policy, axis=1), jnp.sum(stream_policy * stream_...  54.5 us
  transfers between devices with their start and end apart: 10, of which 9 were waited for; matrix products, arithmetic and copies ran while one was open for 3% of the time, Pallas kernels for 0%

commit v1 on v0

v1 whole, which is shorter than its diff:
```python
import functools

import jax
import jax.numpy as jnp
from jax import lax
from jax.experimental import pallas as pl
from jax.experimental.pallas import tpu as pltpu
from jax.sharding import PartitionSpec as P

MESH = pl.DeviceIdType.MESH
EPS = 1e-05
SIDE = 4
SUBS = 2
SUM_TYPE = jnp.float32
HIGH = lax.Precision.HIGHEST
f32 = jnp.float32
bf16 = jnp.bfloat16


def remote(src, dst, send_sem, recv_sem, device):
    return pltpu.make_async_remote_copy(
        src_ref=src,
        dst_ref=dst,
        send_sem=send_sem,
        recv_sem=recv_sem,
        device_id=device,
        device_id_type=MESH,
    )


def add_up(parts):
    while len(parts) > 1:
        parts = [
            parts[i] + parts[i + 1] if i + 1 < len(parts) else parts[i]
            for i in range(0, len(parts), 2)
        ]
    return parts[0]


def normed_tiles(tiles, gain, width):
    center = jnp.sum(add_up(tiles), axis=1, keepdims=True) / width
    tiles = [tile - center for tile in tiles]
    spread = jnp.sum(add_up([tile * tile for tile in tiles]), axis=1, keepdims=True) / width
    scale = lax.rsqrt(spread + EPS)
    return [
        (tile * scale * gain[:, i * 128 : (i + 1) * 128]).astype(bf16) for i, tile in enumerate(tiles)
    ]


def kernel(
    nz,
    hidden_p,
    hidden_r,
    ffn_gain_p,
    ffn_gain_r,
    up_p,
    up_r,
    down_p,
    down_r,
    final_gain_p,
    final_gain_r,
    out_p,
    out_r,
    plan_row,
    plan_cols,
    lengths,
    targets,
    token_diff,
    seq_diff,
    halves,
    feats,
    normed_in,
    up,
    down,
    out,
    partial,
    sums_out,
    sums_in,
    normed_out,
    logits,
    columns,
    wanted,
    target_col,
    select,
    stats,
    lane_lp,
    other_lp,
    diffs,
    local_sem,
    swap_send,
    swap_recv,
    gather_send,
    gather_recv,
    sum_send,
    sum_recv,
    spread_send,
    spread_recv,
    near_send,
    near_recv,
    far_send,
    far_recv,
    target_send,
    target_recv,
    stat_send,
    stat_recv,
    pair_send,
    pair_recv,
    diff_send,
    diff_recv,
):
    dp = lax.axis_index("dp")
    mp = lax.axis_index("mp")
    z, core = mp // 2, mp % 2
    x, y = dp // SIDE, dp % SIDE
    ndp = SIDE * SIDE
    tokens, width = normed_out.shape
    nfeat = width // 128
    own_tokens = tokens // nz
    units = up_p.shape[1]
    vocab = out_p.shape[1]
    depth = out_p.shape[0]
    piece = depth // 2
    quarter = piece // 2
    waits = []

    def z_peer(step):
        return (dp, ((z + step + nz) % nz) * 2 + core)

    def xy_peer(axis, step):
        if axis == 0:
            return (((x + step + SIDE) % SIDE) * SIDE + y, mp)
        return (x * SIDE + (y + step + SIDE) % SIDE, mp)

    sibling = (dp, z * 2 + 1 - core)

    def send(copy):
        copy.start()
        waits.append(copy)

    barrier = pltpu.get_barrier_semaphore()
    greeted = [sibling, z_peer(1), z_peer(-1)]
    greeted += [xy_peer(axis, step) for axis in (0, 1) for step in (1, -1)]
    for device in greeted:
        pl.semaphore_signal(barrier, inc=1, device_id=device, device_id_type=MESH)
    pl.semaphore_wait(barrier, len(greeted))

    own_rows = pl.ds(pl.multiple_of(dp * depth, depth), depth)

    def places(c):
        return (
            halves.at[c],
            out.at[own_rows, c * vocab : (c + 1) * vocab],
            up.at[:, c * units : (c + 1) * units],
            down.at[c * units : (c + 1) * units, :],
        )

    policy = (hidden_p, out_p, up_p, down_p)
    refer = (hidden_r, out_r, up_r, down_r)
    for c in (0, 1):

        @pl.when(core == c)
        def _(c=c):
            mine, theirs = (policy, refer) if c == 0 else (refer, policy)
            for i, place in enumerate(places(c)):
                remote(theirs[i], place, swap_send.at[i], swap_recv.at[i], sibling).start()
                pltpu.make_async_copy(mine[i], place, local_sem.at[i]).start()

    def swap_wait(i):
        for c in (0, 1):

            @pl.when(core == c)
            def _(c=c):
                mine, theirs = (policy, refer) if c == 0 else (refer, policy)
                remote(
                    theirs[i], places(1 - c)[i], swap_send.at[i], swap_recv.at[i], sibling
                ).wait_recv()
                pltpu.make_async_copy(mine[i], places(c)[i], local_sem.at[i]).wait()

    def swap_done(i):
        for c in (0, 1):

            @pl.when(core == c)
            def _(c=c):
                theirs = refer if c == 0 else policy
                remote(
                    theirs[i], places(c)[i], swap_send.at[i], swap_recv.at[i], sibling
                ).wait_send()

    plus, minus = nz // 2, nz // 2 - 1

    def ring_gather(block, send_sem, recv_sem, hooks):
        for k in range(plus + 1):
            for sub in range(SUBS):
                for way, hops, step in ((0, plus, 1), (1, minus, -1)):
                    if 1 <= k <= hops:
                        arrived = block((z - step * k + nz) % nz, sub)
                        remote(
                            arrived,
                            arrived,
                            send_sem.at[way, k - 1, sub],
                            recv_sem.at[way, k - 1, sub],
                            z_peer(step),
                        ).wait_recv()
                    if k < hops:
                        held = block((z - step * k + nz) % nz, sub)
                        send(
                            remote(
                                held,
                                held,
                                send_sem.at[way, k, sub],
                                recv_sem.at[way, k, sub],
                                z_peer(step),
                            )
                        )
            if k in hooks:
                hooks[k]()

    def block_rows(h, along, across, part):
        first, second = (along, across) if h == 0 else (across, along)
        start = (first * SIDE + second) * depth + h * piece
        if part is None:
            return out.at[pl.ds(pl.multiple_of(start, piece), piece), :]
        return out.at[pl.ds(pl.multiple_of(start + part * quarter, quarter), quarter), :]

    def place_of(h):
        return (x, y) if h == 0 else (y, x)

    def along_of(h, j):
        return (place_of(h)[0] + (0, -1, 1, 2)[j] + SIDE) % SIDE

    def near(h, way, forward):
        step = (1, -1)[way]
        u, v = place_of(h)
        if forward:
            rows = block_rows(h, (u - step + SIDE) % SIDE, v, way)
        else:
            rows = block_rows(h, u, v, None)
        sem = (h, way, int(forward))
        return remote(rows, rows, near_send.at[sem], near_recv.at[sem], xy_peer(h, step))

    def near_wait(h, way, forward):
        step = (1, -1)[way]
        u, v = place_of(h)
        if forward:
            rows = block_rows(h, (u - 2 * step + SIDE) % SIDE, v, way)
        else:
            rows = block_rows(h, (u - step + SIDE) % SIDE, v, None)
        sem = (h, way, int(forward))
        remote(rows, rows, near_send.at[sem], near_recv.at[sem], xy_peer(h, step)).wait_recv()

    def far(h, j, way, forward):
        step = (1, -1)[way]
        v = place_of(h)[1]
        if forward:
            rows = block_rows(h, along_of(h, j), (v - step + SIDE) % SIDE, way)
        else:
            rows = block_rows(h, along_of(h, j), v, None)
        sem = (h, j, way, int(forward))
        return remote(rows, rows, far_send.at[sem], far_recv.at[sem], xy_peer(1 - h, step))

    def far_wait(h, j, way, forward):
        step = (1, -1)[way]
        v = place_of(h)[1]
        if forward:
            rows = block_rows(h, along_of(h, j), (v - 2 * step + SIDE) % SIDE, way)
        else:
            rows = block_rows(h, along_of(h, j), (v - step + SIDE) % SIDE, None)
        sem = (h, j, way, int(forward))
        remote(rows, rows, far_send.at[sem], far_recv.at[sem], xy_peer(1 - h, step)).wait_recv()

    both = [(h, way) for h in (0, 1) for way in (0, 1)]

    def out_round_0():
        swap_wait(1)
        for h, way in both:
            send(near(h, way, False))
        for h, way in both:
            send(far(h, 0, way, False))

    def out_round_1():
        for h, way in both:
            near_wait(h, way, False)
            send(near(h, way, True))
        for j in (1, 2):
            for h, way in both:
                send(far(h, j, way, False))
        for h, way in both:
            far_wait(h, 0, way, False)
            send(far(h, 0, way, True))

    def out_round_2():
        for h, way in both:
            near_wait(h, way, True)
        for h, way in both:
            send(far(h, 3, way, False))
        for j in (1, 2):
            for h, way in both:
                far_wait(h, j, way, False)
                send(far(h, j, way, True))

    def out_round_3():
        for h, way in both:
            far_wait(h, 3, way, False)
            send(far(h, 3, way, True))

    def out_round_4():
        for j in range(4):
            for h, way in both:
                far_wait(h, j, way, True)

    swap_wait(0)
    feats[z] = jnp.concatenate([halves[0], halves[1]], axis=1)
    sub_tokens = tokens // SUBS

    def feat_block(source, sub):
        return feats.at[source, sub * sub_tokens : (sub + 1) * sub_tokens, :]

    ring_gather(
        feat_block, gather_send, gather_recv, {0: out_round_0, min(6, plus): out_round_1}
    )

    first_gain = jnp.where(core == 0, ffn_gain_p[...], ffn_gain_r[...])
    row_step = 16

    @pl.loop(0, tokens // row_step)
    def _(i):
        rows = pl.ds(pl.multiple_of(i * row_step, row_step), row_step)
        tiles = [feats[k, rows, :].astype(f32) for k in range(nfeat)]
        for k, tile in enumerate(normed_tiles(tiles, first_gain, width)):
            normed_in[rows, k * 128 : (k + 1) * 128] = tile

    swap_wait(2)
    swap_wait(3)
    pre = jnp.dot(normed_in[...], up[...], preferred_element_type=f32)
    active = jax.nn.gelu(pre).astype(bf16)
    partial[...] = jnp.dot(active, down[...], preferred_element_type=f32)

    sub_width = width // SUBS

    def rows_of(chunk):
        return pl.ds(pl.multiple_of(chunk * own_tokens, own_tokens), own_tokens)

    def sum_copy(way, s, sub):
        cols = slice(sub * sub_width, (sub + 1) * sub_width)
        return remote(
            sums_out.at[way, s, :, cols],
            sums_in.at[way, s, :, cols],
            sum_send.at[way, s, sub],
            sum_recv.at[way, s, sub],
            z_peer((1, -1)[way]),
        )

    sum_hooks = {min(4, plus - 1): out_round_2, plus - 1: out_round_3}
    for s in range(plus):
        for sub in range(SUBS):
            cols = slice(sub * sub_width, (sub + 1) * sub_width)
            for way, hops, step in ((0, plus, 1), (1, minus, -1)):
                if s >= hops:
                    continue
                rows = rows_of((z + step * (hops - s) + nz) % nz)
                term = partial[rows, cols]
                if s > 0:
                    sum_copy(way, s - 1, sub).wait_recv()
                    term = term + sums_in[way, s - 1, :, cols].astype(f32)
                sums_out[way, s, :, cols] = term.astype(sums_out.dtype)
                send(sum_copy(way, s, sub))
        if s in sum_hooks:
            sum_hooks[s]()
    for sub in range(SUBS):
        sum_copy(0, plus - 1, sub).wait_recv()
        sum_copy(1, minus - 1, sub).wait_recv()

    second_gain = jnp.where(core == 0, final_gain_p[...], final_gain_r[...])
    mine = rows_of(z)
    tiles = []
    for k in range(nfeat):
        cols = slice(k * 128, (k + 1) * 128)
        total = (
            partial[mine, cols]
            + sums_in[0, plus - 1, :, cols].astype(f32)
            + sums_in[1, minus - 1, :, cols].astype(f32)
        )
        tiles.append(feats[k, mine, :].astype(f32) + total)
    for k, tile in enumerate(normed_tiles(tiles, second_gain, width)):
        normed_out[mine, k * 128 : (k + 1) * 128] = tile

    def out_block(source, sub):
        return normed_out.at[rows_of(source), sub * sub_width : (sub + 1) * sub_width]

    ring_gather(out_block, spread_send, spread_recv, {})
    out_round_4()

    wanted[dp] = targets[...]

    def target_copy(i):
        return remote(
            wanted.at[dp], wanted.at[dp], target_send.at[i], target_recv.at[i], ((dp + i) % ndp, mp)
        )

    for i in range(1, ndp):
        send(target_copy(i))

    block = 256

    @pl.loop(0, 2 * vocab // block)
    def _(i):
        cols = pl.ds(pl.multiple_of(i * block, block), block)
        logits[:, cols] = jnp.dot(normed_out[...], out[:, cols], preferred_element_type=f32)

    slots = plan_cols.shape[0]
    seq = targets.shape[1]
    for i in range(1, ndp):
        place = wanted.at[(dp - i + ndp) % ndp]
        remote(place, place, target_send.at[i], target_recv.at[i], ((dp + i) % ndp, mp)).wait_recv()
    token = lax.broadcasted_iota(jnp.int32, (tokens, ndp * slots), 0)
    lane = lax.broadcasted_iota(jnp.int32, (tokens, ndp * slots), 1)
    own_request = lane == dp * slots + token // seq
    owner_slot = jnp.sum(
        jnp.where(own_request, plan_row[...].astype(f32), 0.0), axis=1, keepdims=True
    )
    slot_hot = jnp.where(lane.astype(f32) == owner_slot, 1.0, 0.0)
    all_targets = wanted[...].astype(f32).reshape(ndp * slots, seq)
    seen = jnp.dot(slot_hot, all_targets, precision=HIGH, preferred_element_type=f32)
    position = lax.broadcasted_iota(jnp.int32, (tokens, seq), 1)
    row = lax.broadcasted_iota(jnp.int32, (tokens, seq), 0)
    target_col[...] = jnp.sum(
        jnp.where(position == row % seq, seen, 0.0), axis=1, keepdims=True
    ).astype(jnp.int32)

    plan = plan_cols[...]
    slot_id = lax.broadcasted_iota(jnp.int32, (slots, slots, ndp), 1) + dp * slots
    hot = jnp.broadcast_to(plan[:, None, :], (slots, slots, ndp)) == slot_id
    select[...] = jnp.where(hot, 1.0, 0.0).reshape(slots * slots, ndp)

    ntile = 2 * vocab // 128

    @pl.loop(0, tokens // row_step)
    def _(i):
        rows = pl.ds(pl.multiple_of(i * row_step, row_step), row_step)
        tiles = [logits[rows, k * 128 : (k + 1) * 128] for k in range(ntile)]
        top = tiles[0]
        for tile in tiles[1:]:
            top = jnp.maximum(top, tile)
        top = jnp.max(top, axis=1, keepdims=True)
        total = jnp.sum(add_up([jnp.exp(tile - top) for tile in tiles]), axis=1, keepdims=True)
        place = lax.broadcasted_iota(jnp.int32, (row_step, 128), 1)
        spot = target_col[rows, :] - z * (2 * vocab)
        hits = add_up(
            [jnp.where(place == spot - k * 128, tile, 0.0) for k, tile in enumerate(tiles)]
        )
        picked = jnp.sum(hits, axis=1, keepdims=True)
        local = top + jnp.log(total)
        columns[rows, :] = jnp.where(place == 0, local, jnp.where(place == 1, picked, 0.0))

    turned = columns[...].T
    ngroup = tokens // 128
    for g in range(ngroup):
        stats[z, g : g + 1, :] = turned[0:1, g * 128 : (g + 1) * 128]
        stats[z, ngroup + g : ngroup + g + 1, :] = turned[1:2, g * 128 : (g + 1) * 128]

    for i in range(1, nz):
        send(remote(stats.at[z], stats.at[z], stat_send.at[i], stat_recv.at[i], z_peer(i)))
    for i in range(1, nz):
        place = stats.at[(z - i + nz) % nz]
        remote(place, place, stat_send.at[i], stat_recv.at[i], z_peer(i)).wait_recv()
    parts = [stats[i] for i in range(nz)]
    sums = [part[:ngroup] for part in parts]
    top = sums[0]
    for part in sums[1:]:
        top = jnp.maximum(top, part)
    total = add_up([jnp.exp(part - top) for part in sums])
    picked = add_up([part[ngroup:] for part in parts])
    lane_lp[...] = picked - (top + jnp.log(total))

    swap = remote(lane_lp, other_lp, pair_send, pair_recv, sibling)
    send(swap)
    swap.wait_recv()
    difference = jnp.where(
        core == 0, lane_lp[...] - other_lp[...], other_lp[...] - lane_lp[...]
    )
    diffs[dp] = difference

    for i in range(1, ndp):
        send(
            remote(
                diffs.at[dp], diffs.at[dp], diff_send.at[i], diff_recv.at[i], ((dp + i) % ndp, mp)
            )
        )
    for i in range(1, ndp):
        place = diffs.at[(dp - i + ndp) % ndp]
        remote(place, place, diff_send.at[i], diff_recv.at[i], ((dp + i) % ndp, mp)).wait_recv()

    per_group = slots // ngroup
    taken = []
    for g in range(ngroup):
        hot = select[g * per_group * slots : (g + 1) * per_group * slots, :]
        got = jnp.dot(hot, diffs[:, g, :], precision=HIGH, preferred_element_type=f32)
        row = lax.broadcasted_iota(jnp.int32, got.shape, 0) // slots
        lane = lax.broadcasted_iota(jnp.int32, got.shape, 1) // seq
        got = jnp.where(row == lane, got, 0.0)
        taken += [got[j * slots : (j + 1) * slots] for j in range(per_group)]
    fold = jnp.where(
        lax.broadcasted_iota(jnp.int32, (128, seq), 0) % seq
        == lax.broadcasted_iota(jnp.int32, (128, seq), 1),
        1.0,
        0.0,
    )
    moved = jnp.dot(add_up(taken), fold, precision=HIGH, preferred_element_type=f32)
    live = lax.broadcasted_iota(jnp.int32, (slots, seq), 1) < lengths[...]
    kept = jnp.where(live, moved, 0.0)
    token_diff[...] = kept
    seq_diff[...] = jnp.sum(kept, axis=1, keepdims=True)

    for i in range(4):
        swap_done(i)
    for copy in waits:
        copy.wait_send()


def local(
    nz,
    hidden_policy,
    hidden_reference,
    ffn_gain_policy,
    ffn_gain_reference,
    up_policy,
    up_reference,
    down_policy,
    down_reference,
    final_gain_policy,
    final_gain_reference,
    out_policy,
    out_reference,
    move_plan,
    lengths,
    targets,
):
    slots, seq, part = hidden_policy.shape
    tokens = slots * seq
    width = up_policy.shape[0]
    units = up_policy.shape[1]
    vocab = out_policy.shape[1]
    ndp = SIDE * SIDE
    own = tokens // nz
    ngroup = tokens // 128
    plus = nz // 2
    any_space = pl.BlockSpec(memory_space=pl.ANY)
    vmem = pl.BlockSpec(memory_space=pltpu.VMEM)
    dma = pltpu.SemaphoreType.DMA
    ring = (2, plus, SUBS)
    token_diff, seq_diff = pl.pallas_call(
        functools.partial(kernel, nz),
        out_shape=(
            jax.ShapeDtypeStruct((slots, seq), f32),
            jax.ShapeDtypeStruct((slots, 1), f32),
        ),
        in_specs=[any_space, any_space, vmem, vmem]
        + [any_space] * 4
        + [vmem, vmem, any_space, any_space]
        + [vmem] * 4,
        out_specs=(vmem, vmem),
        scratch_shapes=[
            pltpu.VMEM((2, tokens, part), bf16),
            pltpu.VMEM((width // 128, tokens, 128), bf16),
            pltpu.VMEM((tokens, width), bf16),
            pltpu.VMEM((width, 2 * units), bf16),
            pltpu.VMEM((2 * units, width), bf16),
            pltpu.VMEM((width, 2 * vocab), bf16),
            pltpu.VMEM((tokens, width), f32),
            pltpu.VMEM((2, plus, own, width), SUM_TYPE),
            pltpu.VMEM((2, plus, own, width), SUM_TYPE),
            pltpu.VMEM((tokens, width), bf16),
            pltpu.VMEM((tokens, 2 * vocab), f32),
            pltpu.VMEM((tokens, 128), f32),
            pltpu.VMEM((ndp, slots, seq), jnp.int32),
            pltpu.VMEM((tokens, 1), jnp.int32),
            pltpu.VMEM((slots * slots, ndp), f32),
            pltpu.VMEM((nz, 2 * ngroup, 128), f32),
            pltpu.VMEM((ngroup, 128), f32),
            pltpu.VMEM((ngroup, 128), f32),
            pltpu.VMEM((ndp, ngroup, 128), f32),
            dma((4,)),
            dma((4,)),
            dma((4,)),
            dma(ring),
            dma(ring),
            dma(ring),
            dma(ring),
            dma(ring),
            dma(ring),
            dma((2, 2, 2)),
            dma((2, 2, 2)),
            dma((2, 4, 2, 2)),
            dma((2, 4, 2, 2)),
            dma((ndp,)),
            dma((ndp,)),
            dma((nz,)),
            dma((nz,)),
            dma,
            dma,
            dma((ndp,)),
            dma((ndp,)),
        ],
        compiler_params=pltpu.CompilerParams(
            collective_id=0, has_side_effects=True, vmem_limit_bytes=48 * 1024 * 1024
        ),
        name="score",
    )(
        hidden_policy.reshape(tokens, part),
        hidden_reference.reshape(tokens, part),
        ffn_gain_policy.reshape(1, width),
        ffn_gain_reference.reshape(1, width),
        up_policy,
        up_reference,
        down_policy,
        down_reference,
        final_gain_policy.reshape(1, width),
        final_gain_reference.reshape(1, width),
        out_policy,
        out_reference,
        move_plan.reshape(1, ndp * slots),
        move_plan.reshape(ndp, slots).T,
        lengths.reshape(slots, 1),
        targets,
    )
    return token_diff, seq_diff.reshape(slots)


def solution(mesh):
    nz = mesh.shape["mp"] // 2
    return jax.shard_map(
        functools.partial(local, nz),
        mesh=mesh,
        in_specs=(
            P("dp", None, "mp"),
            P("dp", None, "mp"),
            P(),
            P(),
            P(None, "mp"),
            P(None, "mp"),
            P("mp", None),
            P("mp", None),
            P(),
            P(),
            P("dp", "mp"),
            P("dp", "mp"),
            P(),
            P("dp"),
            P("dp", None),
        ),
        out_specs=(P("dp", None), P("dp")),
        check_vma=False,
    )
```

time: 812 us -> 142 us (0.17)
  waiting for transfers between devices: 555 us -> 0 us
  blocking collectives: 197 us -> 0 us
  Pallas kernels: 0 us -> 130 us
  matrix products: 15.3 us -> 0 us
  between operations: 15.6 us -> 0.68 us
  starting transfers between devices: 12.4 us -> 0 us
    all_gather x6 -> x0, waiting for transfers between devices: 333 us -> none  [the longest x1 73.1 us: local(): lax.all_gather(out_normed_policy, 'mp', axis=1, tiled=True)]
    reduce_scatter x2 -> x0, waiting for transfers between devices: 212 us -> none  [the longest x1 110 us: local(): lax.psum_scatter(terms[0], 'mp', scatter_dimension=1, tiled=True)]
    psum x3 -> x0, blocking collectives: 151 us -> none  [the longest x1 54.5 us: local(): lax.psum((jnp.sum(stream_policy, axis=1), jnp.sum(stream_policy * stream_...]
    pallas_call x0 -> x1, Pallas kernels: none -> 130 us  [local(): pl.pallas_call(functools.partial(kernel, nz), out_shape=(jax.ShapeDtypeSt...]
    pmax x1 -> x0, blocking collectives: 45.4 us -> none  [local(): lax.pmax((jnp.max(logits_policy, axis=1), jnp.max(logits_reference, axis=...]
    dot_general x9 -> x0, matrix products: 15.3 us -> none  [the longest x1 3.71 us: local(): jnp.dot(full_reference, pieces[1], preferred_element_type=jnp.float32)]
    all_to_all x2 -> x0, starting transfers between devices: 12.1 us -> none  [the longest x1 7.58 us: local(): lax.all_to_all(packed[1], 'dp', split_axis=0, concat_axis=0, tiled=True)]
    unnamed x10 -> x31, local copies, waits for them, and re-layouts: 0.03 us -> 9.6 us
  transfers between devices with their start and end apart: 10 -> 0, of which waited for: 9 -> 0; matrix products, arithmetic and copies ran while one was open for 3% -> 0% of each run, Pallas kernels for 0% -> 0%
where the time goes in v1:
time: 142 us; the launch traced here: 141 us
  Pallas kernels  130 us (92%)
  local copies, waits for them, and re-layouts  9.83 us (7%)
    pallas_call x1, Pallas kernels, local(): pl.pallas_call(functools.partial(kernel, nz), out_shape=(jax.ShapeDtypeSt...  130 us
    unnamed x31, local copies, waits for them, and re-layouts  9.6 us

profile of v1, /device:TPU:1, one launch (start us, length us, event | category | flops | bytes accessed | tf_op | source)
XLA Modules:
  0.0 141.1 jit_solution(13553248462468455454)
XLA Ops:
  0.6 0.0 copy-start.14
  0.6 0.0 copy-start.12
  0.7 0.0 copy-start.13
  0.7 0.6 copy-done.14
  1.3 0.0 copy-start.11
  1.3 0.1 copy.19.lengths
  1.4 0.0 copy-done.13
  1.4 0.0 copy-start.10
  1.4 0.1 reshape.41
  1.5 0.0 copy-start.9
  1.5 0.1 copy.18
  1.5 0.0 copy-done.12
  1.5 0.5 copy-done.11
  2.0 0.1 copy-done.10
  2.1 0.1 copy-done.8
  2.2 0.0 copy-done.9
  2.2 0.0 copy-start
  2.2 1.0 copy-done
  3.2 0.0 copy-start.1
  3.2 1.0 copy-done.1
  4.3 0.0 copy-start.2
  4.3 1.0 copy-done.2
  5.3 0.0 copy-start.3
  5.3 1.0 copy-done.3
  6.3 0.0 copy-start.4
  6.3 0.9 copy-done.4
  7.3 0.9 copy-done.5
  8.2 0.8 copy-done.6
  9.1 0.8 copy-done.7
  9.9 130.0 %score.1 = (f32[16,16]{1,0:T(8,128)S(1)}, f32[16,1]{1,0:T(8,128)S(1)}) custom-call(bf16[256,64]{1,0:T(8,128)(2,1)S(1)} %bitcast.9, bf16[256,64]{1,0:T(8,128)(2,1)S(1)} %bitcast.10, f32[1,2048]{1,0:T(1,128)S(1)} %bitcast.12, f32[1,2048]{1,0:T(1,128)S(1)} %bitcast.13, bf16[2048,128]{1,0:T(8,128)(2,1)S(1)} %copy-done, bf16[2048,128]{1,0:T(8,128)(2,1)S(1)} %copy-done.1, ...), custom_call_target="tpu_custom_call" | custom-call | tf_op jit(solution)/shard_map/score/pallas_call | solution.py:551
  139.9 0.6 reduce
  140.5 0.6 copy.21
  (4 shorter events, 0.0 us)
Async XLA Ops:
  0.6 0.7 copy-start.14
  0.6 0.9 copy-start.12
  0.7 0.7 copy-start.13
  1.3 0.7 copy-start.11
  1.4 0.7 copy-start.10
  1.5 0.7 copy-start.8
  1.5 0.7 copy-start.9
  2.2 1.0 copy-start
  3.2 1.0 copy-start.1
  4.3 1.0 copy-start.2
  5.3 1.0 copy-start.3
  6.3 0.9 copy-start.4
  7.3 0.9 copy-start.5
  8.2 0.8 copy-start.6
  9.1 0.8 copy-start.7

commit v2 on v1

--- a/solution.py
+++ b/solution.py
@@ -11,7 +11,7 @@
 EPS = 1e-05
 SIDE = 4
 SUBS = 2
-SUM_TYPE = jnp.float32
+SUM_TYPE = jnp.bfloat16
 HIGH = lax.Precision.HIGHEST
 f32 = jnp.float32
 bf16 = jnp.bfloat16
@@ -37,14 +37,14 @@
     return parts[0]
 
 
-def normed_tiles(tiles, gain, width):
-    center = jnp.sum(add_up(tiles), axis=1, keepdims=True) / width
-    tiles = [tile - center for tile in tiles]
-    spread = jnp.sum(add_up([tile * tile for tile in tiles]), axis=1, keepdims=True) / width
+def normed_tiles(load, count, gain, width, store):
+    center = jnp.sum(add_up([load(i) for i in range(count)]), axis=1, keepdims=True) / width
+    squares = [jnp.square(load(i) - center) for i in range(count)]
+    spread = jnp.sum(add_up(squares), axis=1, keepdims=True) / width
     scale = lax.rsqrt(spread + EPS)
-    return [
-        (tile * scale * gain[:, i * 128 : (i + 1) * 128]).astype(bf16) for i, tile in enumerate(tiles)
-    ]
+    for i in range(count):
+        tile = (load(i) - center) * scale * gain[:, i * 128 : (i + 1) * 128]
+        store(i, tile.astype(bf16))
 
 
 def kernel(
@@ -61,12 +61,15 @@
     final_gain_r,
     out_p,
     out_r,
-    plan_row,
-    plan_cols,
-    lengths,
+    plan_hbm,
+    lengths_hbm,
     targets,
     token_diff,
     seq_diff,
+    plan_row,
+    lengths,
+    gains,
+    after,
     halves,
     feats,
     normed_in,
@@ -81,6 +84,7 @@
     columns,
     wanted,
     target_col,
+    slot_hot,
     select,
     stats,
     lane_lp,
@@ -114,6 +118,7 @@
     x, y = dp // SIDE, dp % SIDE
     ndp = SIDE * SIDE
     tokens, width = normed_out.shape
+    slots, seq = token_diff.shape
     nfeat = width // 128
     own_tokens = tokens // nz
     units = up_p.shape[1]
@@ -137,13 +142,6 @@
         copy.start()
         waits.append(copy)
 
-    barrier = pltpu.get_barrier_semaphore()
-    greeted = [sibling, z_peer(1), z_peer(-1)]
-    greeted += [xy_peer(axis, step) for axis in (0, 1) for step in (1, -1)]
-    for device in greeted:
-        pl.semaphore_signal(barrier, inc=1, device_id=device, device_id_type=MESH)
-    pl.semaphore_wait(barrier, len(greeted))
-
     own_rows = pl.ds(pl.multiple_of(dp * depth, depth), depth)
 
     def places(c):
@@ -154,27 +152,54 @@
             down.at[c * units : (c + 1) * units, :],
         )
 
-    policy = (hidden_p, out_p, up_p, down_p)
-    refer = (hidden_r, out_r, up_r, down_r)
+    policy = (hidden_p, out_p, up_p, down_p, ffn_gain_p, final_gain_p)
+    refer = (hidden_r, out_r, up_r, down_r, ffn_gain_r, final_gain_r)
+
+    def local_copy(c, i):
+        mine = policy if c == 0 else refer
+        place = gains.at[i - 4] if i >= 4 else places(c)[i]
+        return pltpu.make_async_copy(mine[i], place, local_sem.at[i])
+
+    small_copies = [
+        pltpu.make_async_copy(plan_hbm, plan_row, local_sem.at[6]),
+        pltpu.make_async_copy(lengths_hbm, lengths, local_sem.at[7]),
+        pltpu.make_async_copy(targets, wanted.at[dp], local_sem.at[8]),
+    ]
     for c in (0, 1):
 
         @pl.when(core == c)
         def _(c=c):
-            mine, theirs = (policy, refer) if c == 0 else (refer, policy)
+            for i in range(6):
+                local_copy(c, i).start()
+
+    for copy in small_copies:
+        copy.start()
+
+    barrier = pltpu.get_barrier_semaphore()
+    greeted = [sibling] + [z_peer(step) for step in (1, -1, 2, -2)]
+    greeted += [xy_peer(axis, step) for axis in (0, 1) for step in (1, -1)]
+    for device in greeted:
+        pl.semaphore_signal(barrier, inc=1, device_id=device, device_id_type=MESH)
+    pl.semaphore_wait(barrier, len(greeted))
+
+    for c in (0, 1):
+
+        @pl.when(core == c)
+        def _(c=c):
+            theirs = refer if c == 0 else policy
             for i, place in enumerate(places(c)):
                 remote(theirs[i], place, swap_send.at[i], swap_recv.at[i], sibling).start()
-                pltpu.make_async_copy(mine[i], place, local_sem.at[i]).start()
 
     def swap_wait(i):
         for c in (0, 1):
 
             @pl.when(core == c)
             def _(c=c):
-                mine, theirs = (policy, refer) if c == 0 else (refer, policy)
+                theirs = refer if c == 0 else policy
                 remote(
                     theirs[i], places(1 - c)[i], swap_send.at[i], swap_recv.at[i], sibling
                 ).wait_recv()
-                pltpu.make_async_copy(mine[i], places(c)[i], local_sem.at[i]).wait()
+                local_copy(c, i).wait()
 
     def swap_done(i):
         for c in (0, 1):
@@ -188,32 +213,33 @@
 
     plus, minus = nz // 2, nz // 2 - 1
 
-    def ring_gather(block, send_sem, recv_sem, hooks):
-        for k in range(plus + 1):
+    ways = ((0, plus, 1), (1, minus, -1))
+
+    def tree_gather(block, send_sem, recv_sem, hooks):
+        def copy(way, step, t, sub, held, far):
+            return remote(
+                block((z - step * held + nz) % nz, sub),
+                block((z - step * held + nz) % nz, sub),
+                send_sem.at[way, t - 1, sub],
+                recv_sem.at[way, t - 1, sub],
+                z_peer(step * far),
+            )
+
+        for held in range(0, plus + 1, 2):
             for sub in range(SUBS):
-                for way, hops, step in ((0, plus, 1), (1, minus, -1)):
-                    if 1 <= k <= hops:
-                        arrived = block((z - step * k + nz) % nz, sub)
-                        remote(
-                            arrived,
-                            arrived,
-                            send_sem.at[way, k - 1, sub],
-                            recv_sem.at[way, k - 1, sub],
-                            z_peer(step),
-                        ).wait_recv()
-                    if k < hops:
-                        held = block((z - step * k + nz) % nz, sub)
-                        send(
-                            remote(
-                                held,
-                                held,
-                                send_sem.at[way, k, sub],
-                                recv_sem.at[way, k, sub],
-                                z_peer(step),
-                            )
-                        )
-            if k in hooks:
-                hooks[k]()
+                for way, hops, step in ways:
+                    if 0 < held <= hops:
+                        copy(way, step, held, sub, held, 2).wait_recv()
+                    for far in (2, 1):
+                        if held + far <= hops:
+                            send(copy(way, step, held + far, sub, held, far))
+            if held in hooks:
+                hooks[held]()
+        for t in range(1, plus + 1, 2):
+            for sub in range(SUBS):
+                for way, hops, step in ways:
+                    if t <= hops:
+                        copy(way, step, t, sub, t, 1).wait_recv()
 
     def block_rows(h, along, across, part):
         first, second = (along, across) if h == 0 else (across, along)
@@ -315,19 +341,50 @@
     def feat_block(source, sub):
         return feats.at[source, sub * sub_tokens : (sub + 1) * sub_tokens, :]
 
-    ring_gather(
-        feat_block, gather_send, gather_recv, {0: out_round_0, min(6, plus): out_round_1}
-    )
-
-    first_gain = jnp.where(core == 0, ffn_gain_p[...], ffn_gain_r[...])
-    row_step = 16
+    def index_work():
+        for copy in small_copies:
+            copy.wait()
+        request = lax.broadcasted_iota(jnp.int32, (slots, ndp * slots), 1)
+        order = lax.broadcasted_iota(jnp.int32, (slots, ndp * slots), 0)
+        spread_plan = jnp.where(request % slots == order, plan_row[...], 0).astype(bf16)
+        request = lax.broadcasted_iota(jnp.int32, (ndp * slots, ndp), 0)
+        holder = lax.broadcasted_iota(jnp.int32, (ndp * slots, ndp), 1)
+        owner = jnp.where(request // slots == holder, 1.0, 0.0).astype(bf16)
+        plan = jnp.dot(spread_plan, owner, preferred_element_type=f32)
+        slot_id = lax.broadcasted_iota(jnp.int32, (slots, slots, ndp), 1) + dp * slots
+        hot = jnp.broadcast_to(plan[:, None, :], (slots, slots, ndp)) == slot_id.astype(f32)
+        select[...] = jnp.where(hot, 1.0, 0.0).reshape(slots * slots, ndp)
+        token = lax.broadcasted_iota(jnp.int32, (tokens, ndp * slots), 0)
+        lane = lax.broadcasted_iota(jnp.int32, (tokens, ndp * slots), 1)
+        own_request = lane == dp * slots + token // seq
+        owner_slot = jnp.sum(
+            jnp.where(own_request, plan_row[...].astype(f32), 0.0), axis=1, keepdims=True
+        )
+        slot_hot[...] = jnp.where(lane.astype(f32) == owner_slot, 1.0, 0.0)
+
+    def first_hook():
+        out_round_0()
+        index_work()
+
+    tree_gather(feat_block, gather_send, gather_recv, {0: first_hook, 4: out_round_1})
+
+    for i in (4, 5):
+        for c in (0, 1):
+
+            @pl.when(core == c)
+            def _(c=c, i=i):
+                local_copy(c, i).wait()
+
+    row_step = min(64, tokens)
 
     @pl.loop(0, tokens // row_step)
     def _(i):
         rows = pl.ds(pl.multiple_of(i * row_step, row_step), row_step)
-        tiles = [feats[k, rows, :].astype(f32) for k in range(nfeat)]
-        for k, tile in enumerate(normed_tiles(tiles, first_gain, width)):
+
+        def store(k, tile):
             normed_in[rows, k * 128 : (k + 1) * 128] = tile
+
+        normed_tiles(lambda k: feats[k, rows, :].astype(f32), nfeat, gains[0], width, store)
 
     swap_wait(2)
     swap_wait(3)
@@ -340,65 +397,85 @@
     def rows_of(chunk):
         return pl.ds(pl.multiple_of(chunk * own_tokens, own_tokens), own_tokens)
 
-    def sum_copy(way, s, sub):
+    def sum_copy(way, t, sub):
         cols = slice(sub * sub_width, (sub + 1) * sub_width)
         return remote(
-            sums_out.at[way, s, :, cols],
-            sums_in.at[way, s, :, cols],
-            sum_send.at[way, s, sub],
-            sum_recv.at[way, s, sub],
-            z_peer((1, -1)[way]),
+            sums_out.at[way, t - 1, :, cols],
+            sums_in.at[way, t - 1, :, cols],
+            sum_send.at[way, t - 1, sub],
+            sum_recv.at[way, t - 1, sub],
+            z_peer((1, -1)[way] * (1 if t % 2 else 2)),
         )
 
-    sum_hooks = {min(4, plus - 1): out_round_2, plus - 1: out_round_3}
-    for s in range(plus):
+    def hand_on(t):
         for sub in range(SUBS):
             cols = slice(sub * sub_width, (sub + 1) * sub_width)
-            for way, hops, step in ((0, plus, 1), (1, minus, -1)):
-                if s >= hops:
+            for way, hops, step in ways:
+                if t > hops:
                     continue
-                rows = rows_of((z + step * (hops - s) + nz) % nz)
-                term = partial[rows, cols]
-                if s > 0:
-                    sum_copy(way, s - 1, sub).wait_recv()
-                    term = term + sums_in[way, s - 1, :, cols].astype(f32)
-                sums_out[way, s, :, cols] = term.astype(sums_out.dtype)
-                send(sum_copy(way, s, sub))
-        if s in sum_hooks:
-            sum_hooks[s]()
-    for sub in range(SUBS):
-        sum_copy(0, plus - 1, sub).wait_recv()
-        sum_copy(1, minus - 1, sub).wait_recv()
-
-    second_gain = jnp.where(core == 0, final_gain_p[...], final_gain_r[...])
+                term = partial[rows_of((z + step * t + nz) % nz), cols]
+                if t % 2 == 0:
+                    for behind in (t + 2, t + 1):
+                        if behind <= hops:
+                            sum_copy(way, behind, sub).wait_recv()
+                            term = term + sums_in[way, behind - 1, :, cols].astype(f32)
+                sums_out[way, t - 1, :, cols] = term.astype(sums_out.dtype)
+                send(sum_copy(way, t, sub))
+
+    hand_on(plus)
+    hand_on(plus - 1)
+    for t in range(plus - 2, 0, -2):
+        hand_on(t - 1)
+        hand_on(t)
+        if t == plus - 2:
+            out_round_2()
+    out_round_3()
+    for t in (1, 2):
+        for sub in range(SUBS):
+            for way in (0, 1):
+                sum_copy(way, t, sub).wait_recv()
+
     mine = rows_of(z)
-    tiles = []
     for k in range(nfeat):
         cols = slice(k * 128, (k + 1) * 128)
-        total = (
-            partial[mine, cols]
-            + sums_in[0, plus - 1, :, cols].astype(f32)
-            + sums_in[1, minus - 1, :, cols].astype(f32)
-        )
-        tiles.append(feats[k, mine, :].astype(f32) + total)
-    for k, tile in enumerate(normed_tiles(tiles, second_gain, width)):
+        came = [sums_in[way, t, :, cols].astype(f32) for way in (0, 1) for t in (0, 1)]
+        total = partial[mine, cols] + add_up(came)
+        after[k] = feats[k, mine, :].astype(f32) + total
+
+    def store_out(k, tile):
         normed_out[mine, k * 128 : (k + 1) * 128] = tile
+
+    normed_tiles(lambda k: after[k], nfeat, gains[1], width, store_out)
 
     def out_block(source, sub):
         return normed_out.at[rows_of(source), sub * sub_width : (sub + 1) * sub_width]
 
-    ring_gather(out_block, spread_send, spread_recv, {})
-    out_round_4()
-
-    wanted[dp] = targets[...]
-
-    def target_copy(i):
+    def target_copy(i, source):
         return remote(
-            wanted.at[dp], wanted.at[dp], target_send.at[i], target_recv.at[i], ((dp + i) % ndp, mp)
+            wanted.at[source],
+            wanted.at[source],
+            target_send.at[i],
+            target_recv.at[i],
+            ((dp + i) % ndp, mp),
         )
 
-    for i in range(1, ndp):
-        send(target_copy(i))
+    def send_targets():
+        out_round_4()
+        for i in range(1, ndp):
+            send(target_copy(i, dp))
+
+    def target_work():
+        for i in range(1, ndp):
+            target_copy(i, (dp - i + ndp) % ndp).wait_recv()
+        all_targets = wanted[...].astype(f32).reshape(ndp * slots, seq)
+        seen = jnp.dot(slot_hot[...], all_targets, precision=HIGH, preferred_element_type=f32)
+        position = lax.broadcasted_iota(jnp.int32, (tokens, seq), 1)
+        row = lax.broadcasted_iota(jnp.int32, (tokens, seq), 0)
+        target_col[...] = jnp.sum(
+            jnp.where(position == row % seq, seen, 0.0), axis=1, keepdims=True
+        ).astype(jnp.int32)
+
+    tree_gather(out_block, spread_send, spread_recv, {2: send_targets, 6: target_work})
 
     block = 256
 
@@ -407,49 +484,29 @@
         cols = pl.ds(pl.multiple_of(i * block, block), block)
         logits[:, cols] = jnp.dot(normed_out[...], out[:, cols], preferred_element_type=f32)
 
-    slots = plan_cols.shape[0]
-    seq = targets.shape[1]
-    for i in range(1, ndp):
-        place = wanted.at[(dp - i + ndp) % ndp]
-        remote(place, place, target_send.at[i], target_recv.at[i], ((dp + i) % ndp, mp)).wait_recv()
-    token = lax.broadcasted_iota(jnp.int32, (tokens, ndp * slots), 0)
-    lane = lax.broadcasted_iota(jnp.int32, (tokens, ndp * slots), 1)
-    own_request = lane == dp * slots + token // seq
-    owner_slot = jnp.sum(
-        jnp.where(own_request, plan_row[...].astype(f32), 0.0), axis=1, keepdims=True
-    )
-    slot_hot = jnp.where(lane.astype(f32) == owner_slot, 1.0, 0.0)
-    all_targets = wanted[...].astype(f32).reshape(ndp * slots, seq)
-    seen = jnp.dot(slot_hot, all_targets, precision=HIGH, preferred_element_type=f32)
-    position = lax.broadcasted_iota(jnp.int32, (tokens, seq), 1)
-    row = lax.broadcasted_iota(jnp.int32, (tokens, seq), 0)
-    target_col[...] = jnp.sum(
-        jnp.where(position == row % seq, seen, 0.0), axis=1, keepdims=True
-    ).astype(jnp.int32)
-
-    plan = plan_cols[...]
-    slot_id = lax.broadcasted_iota(jnp.int32, (slots, slots, ndp), 1) + dp * slots
-    hot = jnp.broadcast_to(plan[:, None, :], (slots, slots, ndp)) == slot_id
-    select[...] = jnp.where(hot, 1.0, 0.0).reshape(slots * slots, ndp)
-
     ntile = 2 * vocab // 128
 
     @pl.loop(0, tokens // row_step)
     def _(i):
         rows = pl.ds(pl.multiple_of(i * row_step, row_step), row_step)
-        tiles = [logits[rows, k * 128 : (k + 1) * 128] for k in range(ntile)]
-        top = tiles[0]
-        for tile in tiles[1:]:
-            top = jnp.maximum(top, tile)
+
+        def load(k):
+            return logits[rows, k * 128 : (k + 1) * 128]
+
+        top = load(0)
+        for k in range(1, ntile):
+            top = jnp.maximum(top, load(k))
         top = jnp.max(top, axis=1, keepdims=True)
-        total = jnp.sum(add_up([jnp.exp(tile - top) for tile in tiles]), axis=1, keepdims=True)
         place = lax.broadcasted_iota(jnp.int32, (row_step, 128), 1)
-        spot = target_col[rows, :] - z * (2 * vocab)
-        hits = add_up(
-            [jnp.where(place == spot - k * 128, tile, 0.0) for k, tile in enumerate(tiles)]
-        )
+        spot = target_col[rows, :] - z * (2 * vocab) - place
+        total = jnp.zeros((row_step, 128), f32)
+        hits = jnp.zeros((row_step, 128), f32)
+        for k in range(ntile):
+            tile = load(k)
+            total = total + jnp.exp(tile - top)
+            hits = hits + jnp.where(spot == k * 128, tile, 0.0)
+        local = top + jnp.log(jnp.sum(total, axis=1, keepdims=True))
         picked = jnp.sum(hits, axis=1, keepdims=True)
-        local = top + jnp.log(total)
         columns[rows, :] = jnp.where(place == 0, local, jnp.where(place == 1, picked, 0.0))
 
     turned = columns[...].T
@@ -506,10 +563,14 @@
         0.0,
     )
     moved = jnp.dot(add_up(taken), fold, precision=HIGH, preferred_element_type=f32)
-    live = lax.broadcasted_iota(jnp.int32, (slots, seq), 1) < lengths[...]
+    here = lax.broadcasted_iota(jnp.int32, (slots, slots), 0)
+    there = lax.broadcasted_iota(jnp.int32, (slots, slots), 1)
+    long = jnp.sum(jnp.where(here == there, lengths[...].astype(f32), 0.0), axis=1, keepdims=True)
+    live = lax.broadcasted_iota(jnp.int32, (slots, seq), 1).astype(f32) < long
     kept = jnp.where(live, moved, 0.0)
     token_diff[...] = kept
-    seq_diff[...] = jnp.sum(kept, axis=1, keepdims=True)
+    in_all = jnp.sum(kept, axis=1, keepdims=True)
+    seq_diff[...] = jnp.sum(jnp.where(here == there, in_all, 0.0), axis=0, keepdims=True)
 
     for i in range(4):
         swap_done(i)
@@ -552,14 +613,15 @@
         functools.partial(kernel, nz),
         out_shape=(
             jax.ShapeDtypeStruct((slots, seq), f32),
-            jax.ShapeDtypeStruct((slots, 1), f32),
+            jax.ShapeDtypeStruct((1, slots), f32),
         ),
-        in_specs=[any_space, any_space, vmem, vmem]
-        + [any_space] * 4
-        + [vmem, vmem, any_space, any_space]
-        + [vmem] * 4,
+        in_specs=[any_space] * 15,
         out_specs=(vmem, vmem),
         scratch_shapes=[
+            pltpu.VMEM((1, ndp * slots), jnp.int32),
+            pltpu.VMEM((1, slots), jnp.int32),
+            pltpu.VMEM((2, 1, width), f32),
+            pltpu.VMEM((width // 128, own, 128), f32),
             pltpu.VMEM((2, tokens, part), bf16),
             pltpu.VMEM((width // 128, tokens, 128), bf16),
             pltpu.VMEM((tokens, width), bf16),
@@ -574,12 +636,13 @@
             pltpu.VMEM((tokens, 128), f32),
             pltpu.VMEM((ndp, slots, seq), jnp.int32),
             pltpu.VMEM((tokens, 1), jnp.int32),
+            pltpu.VMEM((tokens, ndp * slots), f32),
             pltpu.VMEM((slots * slots, ndp), f32),
             pltpu.VMEM((nz, 2 * ngroup, 128), f32),
             pltpu.VMEM((ngroup, 128), f32),
             pltpu.VMEM((ngroup, 128), f32),
             pltpu.VMEM((ndp, ngroup, 128), f32),
-            dma((4,)),
+            dma((9,)),
             dma((4,)),
             dma((4,)),
             dma(ring),
@@ -602,7 +665,7 @@
             dma((ndp,)),
         ],
         compiler_params=pltpu.CompilerParams(
-            collective_id=0, has_side_effects=True, vmem_limit_bytes=48 * 1024 * 1024
+            collective_id=0, has_side_effects=True, vmem_limit_bytes=60 * 1024 * 1024
         ),
         name="score",
     )(
@@ -619,8 +682,7 @@
         out_policy,
         out_reference,
         move_plan.reshape(1, ndp * slots),
-        move_plan.reshape(ndp, slots).T,
-        lengths.reshape(slots, 1),
+        lengths.reshape(1, slots),
         targets,
     )
     return token_diff, seq_diff.reshape(slots)

time: 142 us -> 101 us (0.71)
  Pallas kernels: 130 us -> 98 us
  local copies, waits for them, and re-layouts: 9.83 us -> 1.81 us
    pallas_call x1, Pallas kernels: 130 us -> 98 us  [local(): pl.pallas_call(functools.partial(kernel, nz), out_shape=(jax.ShapeDtypeSt...]
    unnamed x31 -> x4, local copies, waits for them, and re-layouts: 9.6 us -> 1.81 us
where the time goes in v2:
time: 101 us; the launch traced here: 100 us
  Pallas kernels  98 us (97%)
  local copies, waits for them, and re-layouts  1.81 us (2%)
    pallas_call x1, Pallas kernels, local(): pl.pallas_call(functools.partial(kernel, nz), out_shape=(jax.ShapeDtypeSt...  98 us

profile of v2, /device:TPU:1, one launch (start us, length us, event | category | flops | bytes accessed | tf_op | source)
XLA Modules:
  0.0 100.5 jit_solution(11665029225118901570)
XLA Ops:
  0.6 98.0 %score.1 = (f32[16,16]{1,0:T(8,128)}, f32[1,16]{1,0:T(1,128)}) custom-call(bf16[256,64]{1,0:T(8,128)(2,1)} %bitcast.9, bf16[256,64]{1,0:T(8,128)(2,1)} %bitcast.10, f32[1,2048]{1,0:T(1,128)} %bitcast.11, f32[1,2048]{1,0:T(1,128)} %bitcast.12, bf16[2048,128]{1,0:T(8,128)(2,1)} %up_p.1, bf16[2048,128]{1,0:T(8,128)(2,1)} %up_r.1, bf16[128,2048]{1,0:T(8,128)(2,1)} %down_p.1, ...), custom_call_target="tpu_custom_call" | custom-call | tf_op jit(solution)/shard_map/score/pallas_call | solution.py:612
  98.6 0.0 copy-start
  98.7 1.3 %copy.19 = f32[16,16]{1,0:T(8,128)} copy(f32[16,16]{1,0:T(8,128)} %get-tuple-element.8) | data formatting | bytes 2048
  100.0 0.0 copy-done
  100.0 0.5 copy.20
Async XLA Ops:
  98.6 1.3 %copy-start = (f32[1,16]{1,0:T(1,128)S(1)}, f32[1,16]{1,0:T(1,128)}, u32[]{:S(2)}) copy-start(f32[1,16]{1,0:T(1,128)} %get-tuple-element.5) | copy-start | bytes 196

commit v3 on v2

--- a/solution.py
+++ b/solution.py
@@ -87,9 +87,7 @@
     slot_hot,
     select,
     stats,
-    lane_lp,
-    other_lp,
-    diffs,
+    lps,
     local_sem,
     swap_send,
     swap_recv,
@@ -107,10 +105,8 @@
     target_recv,
     stat_send,
     stat_recv,
-    pair_send,
-    pair_recv,
-    diff_send,
-    diff_recv,
+    lp_send,
+    lp_recv,
 ):
     dp = lax.axis_index("dp")
     mp = lax.axis_index("mp")
@@ -128,6 +124,12 @@
     quarter = piece // 2
     waits = []
 
+    far_first_z = sorted(range(1, nz), key=lambda i: -min(i, nz - i))
+    far_first_dp = sorted(
+        range(1, ndp),
+        key=lambda i: -min(i // SIDE, SIDE - i // SIDE) - min(i % SIDE, SIDE - i % SIDE),
+    )
+
     def z_peer(step):
         return (dp, ((z + step + nz) % nz) * 2 + core)
 
@@ -141,6 +143,11 @@
     def send(copy):
         copy.start()
         waits.append(copy)
+
+    def settle(copies):
+        for copy in copies:
+            copy.wait_send()
+        copies.clear()
 
     own_rows = pl.ds(pl.multiple_of(dp * depth, depth), depth)
 
@@ -187,8 +194,7 @@
         @pl.when(core == c)
         def _(c=c):
             theirs = refer if c == 0 else policy
-            for i, place in enumerate(places(c)):
-                remote(theirs[i], place, swap_send.at[i], swap_recv.at[i], sibling).start()
+            remote(theirs[0], places(c)[0], swap_send.at[0], swap_recv.at[0], sibling).start()
 
     def swap_wait(i):
         for c in (0, 1):
@@ -213,33 +219,43 @@
 
     plus, minus = nz // 2, nz // 2 - 1
 
-    ways = ((0, plus, 1), (1, minus, -1))
-
-    def tree_gather(block, send_sem, recv_sem, hooks):
-        def copy(way, step, t, sub, held, far):
-            return remote(
-                block((z - step * held + nz) % nz, sub),
-                block((z - step * held + nz) % nz, sub),
-                send_sem.at[way, t - 1, sub],
-                recv_sem.at[way, t - 1, sub],
-                z_peer(step * far),
-            )
+    half = plus // 2
+    ways = ((0, 1), (1, -1))
+
+    def reach(way, sub):
+        return plus if (sub < (SUBS + 1) // 2) == (way == 0) else minus
+
+    def tree_gather(place, far_place, send_sem, recv_sem, hooks):
+        def arrived(way, step, t, sub):
+            block = place(step, t, sub)
+            sems = send_sem.at[way, t - 1, sub], recv_sem.at[way, t - 1, sub]
+            remote(block, block, *sems, z_peer(step)).wait_recv()
+
+        def wait_odd(first, last):
+            for t in range(first, last, 2):
+                for sub in range(SUBS):
+                    for way, step in ways:
+                        if t <= reach(way, sub):
+                            arrived(way, step, t, sub)
 
         for held in range(0, plus + 1, 2):
             for sub in range(SUBS):
-                for way, hops, step in ways:
+                for way, step in ways:
+                    hops = reach(way, sub)
                     if 0 < held <= hops:
-                        copy(way, step, held, sub, held, 2).wait_recv()
+                        arrived(way, step, held, sub)
                     for far in (2, 1):
-                        if held + far <= hops:
-                            send(copy(way, step, held + far, sub, held, far))
+                        t = held + far
+                        if t <= hops:
+                            sems = send_sem.at[way, t - 1, sub], recv_sem.at[way, t - 1, sub]
+                            block = place(step, held, sub)
+                            there = far_place(step, held, t, sub)
+                            send(remote(block, there, *sems, z_peer(step * far)))
+            if held == half:
+                wait_odd(1, half)
             if held in hooks:
                 hooks[held]()
-        for t in range(1, plus + 1, 2):
-            for sub in range(SUBS):
-                for way, hops, step in ways:
-                    if t <= hops:
-                        copy(way, step, t, sub, t, 1).wait_recv()
+        wait_odd(half + 1, plus + 1)
 
     def block_rows(h, along, across, part):
         first, second = (along, across) if h == 0 else (across, along)
@@ -338,8 +354,16 @@
     feats[z] = jnp.concatenate([halves[0], halves[1]], axis=1)
     sub_tokens = tokens // SUBS
 
-    def feat_block(source, sub):
+    def feat_place(step, t, sub):
+        source = (z - step * t + nz) % nz
         return feats.at[source, sub * sub_tokens : (sub + 1) * sub_tokens, :]
+
+    def feat_far_place(step, held, t, sub):
+        return feat_place(step, held, sub)
+
+    def whole_order(row):
+        block = (row // own_tokens + (z + nz - half)) % nz
+        return block * own_tokens + row % own_tokens
 
     def index_work():
         for copy in small_copies:
@@ -356,17 +380,27 @@
         select[...] = jnp.where(hot, 1.0, 0.0).reshape(slots * slots, ndp)
         token = lax.broadcasted_iota(jnp.int32, (tokens, ndp * slots), 0)
         lane = lax.broadcasted_iota(jnp.int32, (tokens, ndp * slots), 1)
-        own_request = lane == dp * slots + token // seq
+        own_request = lane == dp * slots + whole_order(token) // seq
         owner_slot = jnp.sum(
             jnp.where(own_request, plan_row[...].astype(f32), 0.0), axis=1, keepdims=True
         )
         slot_hot[...] = jnp.where(lane.astype(f32) == owner_slot, 1.0, 0.0)
 
     def first_hook():
+        for c in (0, 1):
+
+            @pl.when(core == c)
+            def _(c=c):
+                theirs = refer if c == 0 else policy
+                for i, place in enumerate(places(c)):
+                    if i:
+                        remote(theirs[i], place, swap_send.at[i], swap_recv.at[i], sibling).start()
+
         out_round_0()
         index_work()
 
-    tree_gather(feat_block, gather_send, gather_recv, {0: first_hook, 4: out_round_1})
+    hooks = {0: first_hook, half: out_round_1}
+    tree_gather(feat_place, feat_far_place, gather_send, gather_recv, hooks)
 
     for i in (4, 5):
         for c in (0, 1):
@@ -390,7 +424,6 @@
     swap_wait(3)
     pre = jnp.dot(normed_in[...], up[...], preferred_element_type=f32)
     active = jax.nn.gelu(pre).astype(bf16)
-    partial[...] = jnp.dot(active, down[...], preferred_element_type=f32)
 
     sub_width = width // SUBS
 
@@ -410,7 +443,10 @@
     def hand_on(t):
         for sub in range(SUBS):
             cols = slice(sub * sub_width, (sub + 1) * sub_width)
-            for way, hops, step in ways:
+            if t == plus:
+                partial[:, cols] = jnp.dot(active, down[:, cols], preferred_element_type=f32)
+            for way, step in ways:
+                hops = reach(way, sub)
                 if t > hops:
                     continue
                 term = partial[rows_of((z + step * t + nz) % nz), cols]
@@ -443,52 +479,66 @@
         after[k] = feats[k, mine, :].astype(f32) + total
 
     def store_out(k, tile):
-        normed_out[mine, k * 128 : (k + 1) * 128] = tile
+        normed_out[half * own_tokens : (half + 1) * own_tokens, k * 128 : (k + 1) * 128] = tile
 
     normed_tiles(lambda k: after[k], nfeat, gains[1], width, store_out)
 
-    def out_block(source, sub):
-        return normed_out.at[rows_of(source), sub * sub_width : (sub + 1) * sub_width]
+    def out_place(step, t, sub):
+        slot = (half - step * t + nz) % nz
+        cols = slice(sub * sub_width, (sub + 1) * sub_width)
+        return normed_out.at[slot * own_tokens : (slot + 1) * own_tokens, cols]
+
+    def out_far_place(step, held, t, sub):
+        return out_place(step, t, sub)
 
     def target_copy(i, source):
         return remote(
             wanted.at[source],
             wanted.at[source],
-            target_send.at[i],
-            target_recv.at[i],
+            target_send,
+            target_recv,
             ((dp + i) % ndp, mp),
         )
 
     def send_targets():
         out_round_4()
         for i in range(1, ndp):
-            send(target_copy(i, dp))
+            target_copy(i, dp).start()
+
+    def settle_early():
+        for i in range(4):
+            swap_done(i)
+        settle(early)
 
     def target_work():
-        for i in range(1, ndp):
-            target_copy(i, (dp - i + ndp) % ndp).wait_recv()
+        others = wanted.at[0 : ndp - 1]
+        every = remote(others, others, target_send, target_recv, sibling)
+        every.wait_send()
+        every.wait_recv()
         all_targets = wanted[...].astype(f32).reshape(ndp * slots, seq)
         seen = jnp.dot(slot_hot[...], all_targets, precision=HIGH, preferred_element_type=f32)
         position = lax.broadcasted_iota(jnp.int32, (tokens, seq), 1)
         row = lax.broadcasted_iota(jnp.int32, (tokens, seq), 0)
         target_col[...] = jnp.sum(
-            jnp.where(position == row % seq, seen, 0.0), axis=1, keepdims=True
+            jnp.where(position == whole_order(row) % seq, seen, 0.0), axis=1, keepdims=True
         ).astype(jnp.int32)
 
-    tree_gather(out_block, spread_send, spread_recv, {2: send_targets, 6: target_work})
-
     block = 256
-
-    @pl.loop(0, 2 * vocab // block)
-    def _(i):
-        cols = pl.ds(pl.multiple_of(i * block, block), block)
-        logits[:, cols] = jnp.dot(normed_out[...], out[:, cols], preferred_element_type=f32)
-
     ntile = 2 * vocab // 128
 
-    @pl.loop(0, tokens // row_step)
-    def _(i):
-        rows = pl.ds(pl.multiple_of(i * row_step, row_step), row_step)
+    def score(first, last):
+        rows = slice(first * own_tokens, last * own_tokens)
+
+        @pl.loop(0, 2 * vocab // block)
+        def _(i):
+            cols = pl.ds(pl.multiple_of(i * block, block), block)
+            logits[rows, cols] = jnp.dot(
+                normed_out[rows, :], out[:, cols], preferred_element_type=f32
+            )
+
+    def summarize(first, last):
+        rows = slice(first * own_tokens, last * own_tokens)
+        shape = ((last - first) * own_tokens, 128)
 
         def load(k):
             return logits[rows, k * 128 : (k + 1) * 128]
@@ -497,17 +547,41 @@
         for k in range(1, ntile):
             top = jnp.maximum(top, load(k))
         top = jnp.max(top, axis=1, keepdims=True)
-        place = lax.broadcasted_iota(jnp.int32, (row_step, 128), 1)
+        place = lax.broadcasted_iota(jnp.int32, shape, 1)
         spot = target_col[rows, :] - z * (2 * vocab) - place
-        total = jnp.zeros((row_step, 128), f32)
-        hits = jnp.zeros((row_step, 128), f32)
+        total = jnp.zeros(shape, f32)
+        hits = jnp.zeros(shape, f32)
         for k in range(ntile):
             tile = load(k)
             total = total + jnp.exp(tile - top)
             hits = hits + jnp.where(spot == k * 128, tile, 0.0)
         local = top + jnp.log(jnp.sum(total, axis=1, keepdims=True))
         picked = jnp.sum(hits, axis=1, keepdims=True)
-        columns[rows, :] = jnp.where(place == 0, local, jnp.where(place == 1, picked, 0.0))
+        values = jnp.where(place == 0, local, jnp.where(place == 1, picked, 0.0))
+        for i in range(first, last):
+            block_rows = values[(i - first) * own_tokens : (i - first + 1) * own_tokens]
+            columns[rows_of((z + i + nz - half) % nz), :] = block_rows
+
+    def summarize_all(first, last):
+        for i in range(first, last, 3):
+            summarize(i, min(i + 3, last))
+
+    near_blocks = 2 * half + 1
+
+    def before_far():
+        target_work()
+        summarize_all(0, near_blocks)
+
+    def after_relay():
+        send_targets()
+        settle_early()
+
+    early = list(waits)
+    waits.clear()
+    hooks = {2: after_relay, half: lambda: score(0, near_blocks), plus - 2: before_far}
+    tree_gather(out_place, out_far_place, spread_send, spread_recv, hooks)
+    score(near_blocks, nz)
+    summarize_all(near_blocks, nz)
 
     turned = columns[...].T
     ngroup = tokens // 128
@@ -515,11 +589,13 @@
         stats[z, g : g + 1, :] = turned[0:1, g * 128 : (g + 1) * 128]
         stats[z, ngroup + g : ngroup + g + 1, :] = turned[1:2, g * 128 : (g + 1) * 128]
 
-    for i in range(1, nz):
-        send(remote(stats.at[z], stats.at[z], stat_send.at[i], stat_recv.at[i], z_peer(i)))
-    for i in range(1, nz):
-        place = stats.at[(z - i + nz) % nz]
-        remote(place, place, stat_send.at[i], stat_recv.at[i], z_peer(i)).wait_recv()
+    for i in far_first_z:
+        remote(stats.at[z], stats.at[z], stat_send, stat_recv, z_peer(i)).start()
+    settle(waits)
+    others = stats.at[0 : nz - 1]
+    every = remote(others, others, stat_send, stat_recv, z_peer(1))
+    every.wait_send()
+    every.wait_recv()
     parts = [stats[i] for i in range(nz)]
     sums = [part[:ngroup] for part in parts]
     top = sums[0]
@@ -527,31 +603,25 @@
         top = jnp.maximum(top, part)
     total = add_up([jnp.exp(part - top) for part in sums])
     picked = add_up([part[ngroup:] for part in parts])
-    lane_lp[...] = picked - (top + jnp.log(total))
-
-    swap = remote(lane_lp, other_lp, pair_send, pair_recv, sibling)
-    send(swap)
-    swap.wait_recv()
-    difference = jnp.where(
-        core == 0, lane_lp[...] - other_lp[...], other_lp[...] - lane_lp[...]
-    )
-    diffs[dp] = difference
-
-    for i in range(1, ndp):
-        send(
-            remote(
-                diffs.at[dp], diffs.at[dp], diff_send.at[i], diff_recv.at[i], ((dp + i) % ndp, mp)
-            )
-        )
-    for i in range(1, ndp):
-        place = diffs.at[(dp - i + ndp) % ndp]
-        remote(place, place, diff_send.at[i], diff_recv.at[i], ((dp + i) % ndp, mp)).wait_recv()
+    lps[core * ndp + dp] = picked - (top + jnp.log(total))
+
+    place = lps.at[core * ndp + dp]
+    for step in far_first_dp + [0]:
+        for turn in (0, 1):
+            if step or turn:
+                peer = ((x + step // SIDE) % SIDE) * SIDE + (y + step % SIDE) % SIDE
+                device = (peer, z * 2 + (core + turn) % 2)
+                remote(place, place, lp_send, lp_recv, device).start()
+    others = lps.at[0 : 2 * ndp - 1]
+    every = remote(others, others, lp_send, lp_recv, sibling)
+    every.wait_recv()
 
     per_group = slots // ngroup
     taken = []
     for g in range(ngroup):
         hot = select[g * per_group * slots : (g + 1) * per_group * slots, :]
-        got = jnp.dot(hot, diffs[:, g, :], precision=HIGH, preferred_element_type=f32)
+        between = lps[:ndp, g, :] - lps[ndp:, g, :]
+        got = jnp.dot(hot, between, precision=HIGH, preferred_element_type=f32)
         row = lax.broadcasted_iota(jnp.int32, got.shape, 0) // slots
         lane = lax.broadcasted_iota(jnp.int32, got.shape, 1) // seq
         got = jnp.where(row == lane, got, 0.0)
@@ -572,10 +642,7 @@
     in_all = jnp.sum(kept, axis=1, keepdims=True)
     seq_diff[...] = jnp.sum(jnp.where(here == there, in_all, 0.0), axis=0, keepdims=True)
 
-    for i in range(4):
-        swap_done(i)
-    for copy in waits:
-        copy.wait_send()
+    every.wait_send()
 
 
 def local(
@@ -639,9 +706,7 @@
             pltpu.VMEM((tokens, ndp * slots), f32),
             pltpu.VMEM((slots * slots, ndp), f32),
             pltpu.VMEM((nz, 2 * ngroup, 128), f32),
-            pltpu.VMEM((ngroup, 128), f32),
-            pltpu.VMEM((ngroup, 128), f32),
-            pltpu.VMEM((ndp, ngroup, 128), f32),
+            pltpu.VMEM((2 * ndp, ngroup, 128), f32),
             dma((9,)),
             dma((4,)),
             dma((4,)),
@@ -655,14 +720,12 @@
             dma((2, 2, 2)),
             dma((2, 4, 2, 2)),
             dma((2, 4, 2, 2)),
-            dma((ndp,)),
-            dma((ndp,)),
-            dma((nz,)),
-            dma((nz,)),
             dma,
             dma,
-            dma((ndp,)),
-            dma((ndp,)),
+            dma,
+            dma,
+            dma,
+            dma,
         ],
         compiler_params=pltpu.CompilerParams(
             collective_id=0, has_side_effects=True, vmem_limit_bytes=60 * 1024 * 1024
@@ -685,6 +748,18 @@
         lengths.reshape(1, slots),
         targets,
     )
+    def hand_over(token_in, seq_in, token_out, seq_out):
+        token_out[...] = token_in[...]
+        seq_out[...] = seq_in[...]
+
+    token_diff, seq_diff = pl.pallas_call(
+        hand_over,
+        out_shape=(
+            jax.ShapeDtypeStruct((slots, seq), f32),
+            jax.ShapeDtypeStruct((1, slots), f32),
+        ),
+        name="hand_over",
+    )(token_diff, seq_diff)
     return token_diff, seq_diff.reshape(slots)
 
 

time: 101 us -> 97 us (0.960)
  local copies, waits for them, and re-layouts: 1.81 us -> 0 us
  Pallas kernels: 98 us -> 96.2 us
    pallas_call x1, Pallas kernels: 98 us -> 94.9 us  [local(): pl.pallas_call(functools.partial(kernel, nz), out_shape=(jax.ShapeDtypeSt...]
    unnamed x4 -> x0, local copies, waits for them, and re-layouts: 1.81 us -> none
    pallas_call x0 -> x1, Pallas kernels: none -> 1.3 us  [local(): pl.pallas_call(hand_over, out_shape=(jax.ShapeDtypeStruct((slots, seq), f...]
where the time goes in v3:
time: 97 us; the launch traced here: 96.9 us
  Pallas kernels  96.2 us (99%)
    pallas_call x1, Pallas kernels, local(): pl.pallas_call(functools.partial(kernel, nz), out_shape=(jax.ShapeDtypeSt...  94.9 us

profile of v3, /device:TPU:1, one launch (start us, length us, event | category | flops | bytes accessed | tf_op | source)
XLA Modules:
  0.0 96.9 jit_solution(13617285996973102464)
XLA Ops:
  0.6 94.9 %score.1 = (f32[16,16]{1,0:T(8,128)}, f32[1,16]{1,0:T(1,128)}) custom-call(bf16[256,64]{1,0:T(8,128)(2,1)} %bitcast.9, bf16[256,64]{1,0:T(8,128)(2,1)} %bitcast.10, f32[1,2048]{1,0:T(1,128)} %bitcast.11, f32[1,2048]{1,0:T(1,128)} %bitcast.12, bf16[2048,128]{1,0:T(8,128)(2,1)} %up_p.1, bf16[2048,128]{1,0:T(8,128)(2,1)} %up_r.1, bf16[128,2048]{1,0:T(8,128)(2,1)} %down_p.1, ...), custom_call_target="tpu_custom_call" | custom-call | tf_op jit(solution)/shard_map/score/pallas_call | solution.py:679
  95.6 1.3 %hand_over.1 = (f32[16,16]{1,0:T(8,128)}, f32[1,16]{1,0:T(1,128)}) custom-call(f32[16,16]{1,0:T(8,128)} %get-tuple-element.6.token_in, f32[1,16]{1,0:T(1,128)} %get-tuple-element.7.seq_in), custom_call_target="tpu_custom_call" | custom-call | tf_op jit(solution)/shard_map/hand_over/pallas_call | solution.py:755

commit v4 on v3

--- a/solution.py
+++ b/solution.py
@@ -239,6 +239,7 @@
                             arrived(way, step, t, sub)
 
         for held in range(0, plus + 1, 2):
+            late = []
             for sub in range(SUBS):
                 for way, step in ways:
                     hops = reach(way, sub)
@@ -250,7 +251,13 @@
                             sems = send_sem.at[way, t - 1, sub], recv_sem.at[way, t - 1, sub]
                             block = place(step, held, sub)
                             there = far_place(step, held, t, sub)
-                            send(remote(block, there, *sems, z_peer(step * far)))
+                            copy = remote(block, there, *sems, z_peer(step * far))
+                            if far == 1:
+                                late.append(copy)
+                            else:
+                                send(copy)
+            for copy in late:
+                send(copy)
             if held == half:
                 wait_odd(1, half)
             if held in hooks:
@@ -458,11 +465,15 @@
                 sums_out[way, t - 1, :, cols] = term.astype(sums_out.dtype)
                 send(sum_copy(way, t, sub))
 
-    hand_on(plus)
-    hand_on(plus - 1)
-    for t in range(plus - 2, 0, -2):
-        hand_on(t - 1)
+    for t in range(plus, 0, -2):
         hand_on(t)
+        if t == plus:
+            hand_on(t - 1)
+            hand_on(t - 3)
+        elif t > 4:
+            hand_on(t - 3)
+        elif t == 4:
+            hand_on(1)
         if t == plus - 2:
             out_round_2()
     out_round_3()

time: 97 us -> 96.2 us (level)
  no operation moved by 1% of the time
where the time goes in v4:
time: 96.2 us; the launch traced here: 96 us
  Pallas kernels  95.4 us (99%)
    pallas_call x1, Pallas kernels, local(): pl.pallas_call(functools.partial(kernel, nz), out_shape=(jax.ShapeDtypeSt...  94.1 us

profile of v4, /device:TPU:1, one launch (start us, length us, event | category | flops | bytes accessed | tf_op | source)
XLA Modules:
  0.0 96.0 jit_solution(8793283786408513841)
XLA Ops:
  0.6 94.1 %score.1 = (f32[16,16]{1,0:T(8,128)}, f32[1,16]{1,0:T(1,128)}) custom-call(bf16[256,64]{1,0:T(8,128)(2,1)} %bitcast.9, bf16[256,64]{1,0:T(8,128)(2,1)} %bitcast.10, f32[1,2048]{1,0:T(1,128)} %bitcast.11, f32[1,2048]{1,0:T(1,128)} %bitcast.12, bf16[2048,128]{1,0:T(8,128)(2,1)} %up_p.1, bf16[2048,128]{1,0:T(8,128)(2,1)} %up_r.1, bf16[128,2048]{1,0:T(8,128)(2,1)} %down_p.1, ...), custom_call_target="tpu_custom_call" | custom-call | tf_op jit(solution)/shard_map/score/pallas_call | solution.py:690
  94.7 1.3 %hand_over.1 = (f32[16,16]{1,0:T(8,128)}, f32[1,16]{1,0:T(1,128)}) custom-call(f32[16,16]{1,0:T(8,128)} %get-tuple-element.6.token_in, f32[1,16]{1,0:T(1,128)} %get-tuple-element.7.seq_in), custom_call_target="tpu_custom_call" | custom-call | tf_op jit(solution)/shard_map/hand_over/pallas_call | solution.py:766

commit v5 on v3

--- a/solution.py
+++ b/solution.py
@@ -71,6 +71,8 @@
     gains,
     after,
     halves,
+    outbox,
+    folded,
     feats,
     normed_in,
     up,
@@ -153,7 +155,7 @@
 
     def places(c):
         return (
-            halves.at[c],
+            folded.at[z, c],
             out.at[own_rows, c * vocab : (c + 1) * vocab],
             up.at[:, c * units : (c + 1) * units],
             down.at[c * units : (c + 1) * units, :],
@@ -164,8 +166,12 @@
 
     def local_copy(c, i):
         mine = policy if c == 0 else refer
-        place = gains.at[i - 4] if i >= 4 else places(c)[i]
+        place = halves.at[0] if i == 0 else gains.at[i - 4] if i >= 4 else places(c)[i]
         return pltpu.make_async_copy(mine[i], place, local_sem.at[i])
+
+    def other_copy(c):
+        theirs = refer if c == 0 else policy
+        return pltpu.make_async_copy(theirs[0], halves.at[1], local_sem.at[9])
 
     small_copies = [
         pltpu.make_async_copy(plan_hbm, plan_row, local_sem.at[6]),
@@ -176,6 +182,7 @@
 
         @pl.when(core == c)
         def _(c=c):
+            other_copy(c).start()
             for i in range(6):
                 local_copy(c, i).start()
 
@@ -187,14 +194,26 @@
     greeted += [xy_peer(axis, step) for axis in (0, 1) for step in (1, -1)]
     for device in greeted:
         pl.semaphore_signal(barrier, inc=1, device_id=device, device_id_type=MESH)
-    pl.semaphore_wait(barrier, len(greeted))
-
     for c in (0, 1):
 
         @pl.when(core == c)
         def _(c=c):
-            theirs = refer if c == 0 else policy
-            remote(theirs[0], places(c)[0], swap_send.at[0], swap_recv.at[0], sibling).start()
+            local_copy(c, 0).wait()
+            other_copy(c).wait()
+
+    def fold(i):
+        half_tokens = tokens // 2
+        return jnp.concatenate([halves[i, :half_tokens, :], halves[i, half_tokens:, :]], axis=1)
+
+    outbox[...] = fold(1)
+    folded[z, core] = fold(0)
+    pl.semaphore_wait(barrier, len(greeted))
+
+    for c in (0, 1):
+
+        @pl.when(core == c)
+        def _(c=c):
+            remote(outbox, places(c)[0], swap_send.at[0], swap_recv.at[0], sibling).start()
 
     def swap_wait(i):
         for c in (0, 1):
@@ -203,9 +222,10 @@
             def _(c=c):
                 theirs = refer if c == 0 else policy
                 remote(
-                    theirs[i], places(1 - c)[i], swap_send.at[i], swap_recv.at[i], sibling
+                    theirs[i] if i else outbox, places(1 - c)[i], swap_send.at[i], swap_recv.at[i], sibling
                 ).wait_recv()
-                local_copy(c, i).wait()
+                if i:
+                    local_copy(c, i).wait()
 
     def swap_done(i):
         for c in (0, 1):
@@ -214,7 +234,7 @@
             def _(c=c):
                 theirs = refer if c == 0 else policy
                 remote(
-                    theirs[i], places(c)[i], swap_send.at[i], swap_recv.at[i], sibling
+                    theirs[i] if i else outbox, places(c)[i], swap_send.at[i], swap_recv.at[i], sibling
                 ).wait_send()
 
     plus, minus = nz // 2, nz // 2 - 1
@@ -225,7 +245,7 @@
     def reach(way, sub):
         return plus if (sub < (SUBS + 1) // 2) == (way == 0) else minus
 
-    def tree_gather(place, far_place, send_sem, recv_sem, hooks):
+    def tree_gather(place, far_place, send_sem, recv_sem, hooks, between=None):
         def arrived(way, step, t, sub):
             block = place(step, t, sub)
             sems = send_sem.at[way, t - 1, sub], recv_sem.at[way, t - 1, sub]
@@ -239,7 +259,13 @@
                             arrived(way, step, t, sub)
 
         for held in range(0, plus + 1, 2):
+            late = []
             for sub in range(SUBS):
+                if held == 0 and sub == 1 and between is not None:
+                    for copy in late:
+                        send(copy)
+                    late = []
+                    between()
                 for way, step in ways:
                     hops = reach(way, sub)
                     if 0 < held <= hops:
@@ -250,7 +276,13 @@
                             sems = send_sem.at[way, t - 1, sub], recv_sem.at[way, t - 1, sub]
                             block = place(step, held, sub)
                             there = far_place(step, held, t, sub)
-                            send(remote(block, there, *sems, z_peer(step * far)))
+                            copy = remote(block, there, *sems, z_peer(step * far))
+                            if far == 1:
+                                late.append(copy)
+                            else:
+                                send(copy)
+            for copy in late:
+                send(copy)
             if held == half:
                 wait_odd(1, half)
             if held in hooks:
@@ -350,16 +382,27 @@
             for h, way in both:
                 far_wait(h, j, way, True)
 
-    swap_wait(0)
-    feats[z] = jnp.concatenate([halves[0], halves[1]], axis=1)
-    sub_tokens = tokens // SUBS
+    def other_half():
+        swap_wait(0)
 
     def feat_place(step, t, sub):
-        source = (z - step * t + nz) % nz
-        return feats.at[source, sub * sub_tokens : (sub + 1) * sub_tokens, :]
+        return folded.at[(z - step * t + nz) % nz, (core + sub) % 2]
 
     def feat_far_place(step, held, t, sub):
         return feat_place(step, held, sub)
+
+    def unfold(first, last):
+        part = halves.shape[2]
+        half_tokens = tokens // 2
+        for t in range(first, last):
+            for step in (1, -1):
+                if t <= (plus if step == 1 else minus) and (t or step == 1):
+                    source = (z - step * t + nz) % nz
+                    sides = [folded[source, c] for c in (0, 1)]
+                    for i in (0, 1):
+                        feats[source, i * half_tokens : (i + 1) * half_tokens, :] = jnp.concatenate(
+                            [side[:, i * part : (i + 1) * part] for side in sides], axis=1
+                        )
 
     def whole_order(row):
         block = (row // own_tokens + (z + nz - half)) % nz
@@ -399,8 +442,9 @@
         out_round_0()
         index_work()
 
-    hooks = {0: first_hook, half: out_round_1}
-    tree_gather(feat_place, feat_far_place, gather_send, gather_recv, hooks)
+    hooks = {0: first_hook, half: lambda: unfold(0, half + 1), plus - 2: out_round_1}
+    tree_gather(feat_place, feat_far_place, gather_send, gather_recv, hooks, other_half)
+    unfold(half + 1, plus + 1)
 
     for i in (4, 5):
         for c in (0, 1):
@@ -465,7 +509,6 @@
         hand_on(t)
         if t == plus - 2:
             out_round_2()
-    out_round_3()
     for t in (1, 2):
         for sub in range(SUBS):
             for way in (0, 1):
@@ -578,7 +621,12 @@
 
     early = list(waits)
     waits.clear()
-    hooks = {2: after_relay, half: lambda: score(0, near_blocks), plus - 2: before_far}
+    hooks = {
+        0: out_round_3,
+        2: after_relay,
+        half: lambda: score(0, near_blocks),
+        plus - 2: before_far,
+    }
     tree_gather(out_place, out_far_place, spread_send, spread_recv, hooks)
     score(near_blocks, nz)
     summarize_all(near_blocks, nz)
@@ -690,6 +738,8 @@
             pltpu.VMEM((2, 1, width), f32),
             pltpu.VMEM((width // 128, own, 128), f32),
             pltpu.VMEM((2, tokens, part), bf16),
+            pltpu.VMEM((tokens // 2, 2 * part), bf16),
+            pltpu.VMEM((nz, 2, tokens // 2, 128), bf16),
             pltpu.VMEM((width // 128, tokens, 128), bf16),
             pltpu.VMEM((tokens, width), bf16),
             pltpu.VMEM((width, 2 * units), bf16),
@@ -707,7 +757,7 @@
             pltpu.VMEM((slots * slots, ndp), f32),
             pltpu.VMEM((nz, 2 * ngroup, 128), f32),
             pltpu.VMEM((2 * ndp, ngroup, 128), f32),
-            dma((9,)),
+            dma((10,)),
             dma((4,)),
             dma((4,)),
             dma(ring),

time: 97 us -> 95.5 us (0.985)
  Pallas kernels: 96.2 us -> 94.6 us
    pallas_call x1, Pallas kernels: 94.9 us -> 93.3 us  [local(): pl.pallas_call(functools.partial(kernel, nz), out_shape=(jax.ShapeDtypeSt...]
where the time goes in v5:
time: 95.5 us; the launch traced here: 95.3 us
  Pallas kernels  94.6 us (99%)
    pallas_call x1, Pallas kernels, local(): pl.pallas_call(functools.partial(kernel, nz), out_shape=(jax.ShapeDtypeSt...  93.3 us

profile of v5, /device:TPU:1, one launch (start us, length us, event | category | flops | bytes accessed | tf_op | source)
XLA Modules:
  0.0 95.3 jit_solution(14538940401033024287)
XLA Ops:
  0.6 93.3 %score.1 = (f32[16,16]{1,0:T(8,128)}, f32[1,16]{1,0:T(1,128)}) custom-call(bf16[256,64]{1,0:T(8,128)(2,1)} %bitcast.9, bf16[256,64]{1,0:T(8,128)(2,1)} %bitcast.10, f32[1,2048]{1,0:T(1,128)} %bitcast.11, f32[1,2048]{1,0:T(1,128)} %bitcast.12, bf16[2048,128]{1,0:T(8,128)(2,1)} %up_p.1, bf16[2048,128]{1,0:T(8,128)(2,1)} %up_r.1, bf16[128,2048]{1,0:T(8,128)(2,1)} %down_p.1, ...), custom_call_target="tpu_custom_call" | custom-call | tf_op jit(solution)/shard_map/score/pallas_call | solution.py:727
  94.0 1.3 %hand_over.1 = (f32[16,16]{1,0:T(8,128)}, f32[1,16]{1,0:T(1,128)}) custom-call(f32[16,16]{1,0:T(8,128)} %get-tuple-element.6.token_in, f32[1,16]{1,0:T(1,128)} %get-tuple-element.7.seq_in), custom_call_target="tpu_custom_call" | custom-call | tf_op jit(solution)/shard_map/hand_over/pallas_call | solution.py:805

commit v6 on v5

--- a/solution.py
+++ b/solution.py
@@ -453,7 +453,7 @@
             def _(c=c, i=i):
                 local_copy(c, i).wait()
 
-    row_step = min(64, tokens)
+    row_step = min(128, tokens)
 
     @pl.loop(0, tokens // row_step)
     def _(i):
@@ -503,12 +503,16 @@
                 send(sum_copy(way, t, sub))
 
     hand_on(plus)
-    hand_on(plus - 1)
-    for t in range(plus - 2, 0, -2):
-        hand_on(t - 1)
+    for t in range(plus - 1, 2, -2):
         hand_on(t)
-        if t == plus - 2:
+        if t == plus - 5:
+            hand_on(plus - 2)
             out_round_2()
+    for t in range(plus - 4, 0, -2):
+        hand_on(t)
+        if t == plus - 4:
+            hand_on(1)
+
     for t in (1, 2):
         for sub in range(SUBS):
             for way in (0, 1):

time: 95.5 us -> 95 us (level)
  no operation moved by 1% of the time
where the time goes in v6:
time: 95 us; the launch traced here: 94.8 us
  Pallas kernels  94.1 us (99%)
    pallas_call x1, Pallas kernels, local(): pl.pallas_call(functools.partial(kernel, nz), out_shape=(jax.ShapeDtypeSt...  92.8 us

profile of v6, /device:TPU:1, one launch (start us, length us, event | category | flops | bytes accessed | tf_op | source)
XLA Modules:
  0.0 94.8 jit_solution(9734601170382842915)
XLA Ops:
  0.6 92.8 %score.1 = (f32[16,16]{1,0:T(8,128)}, f32[1,16]{1,0:T(1,128)}) custom-call(bf16[256,64]{1,0:T(8,128)(2,1)} %bitcast.9, bf16[256,64]{1,0:T(8,128)(2,1)} %bitcast.10, f32[1,2048]{1,0:T(1,128)} %bitcast.11, f32[1,2048]{1,0:T(1,128)} %bitcast.12, bf16[2048,128]{1,0:T(8,128)(2,1)} %up_p.1, bf16[2048,128]{1,0:T(8,128)(2,1)} %up_r.1, bf16[128,2048]{1,0:T(8,128)(2,1)} %down_p.1, ...), custom_call_target="tpu_custom_call" | custom-call | tf_op jit(solution)/shard_map/score/pallas_call | solution.py:731
  93.5 1.3 %hand_over.1 = (f32[16,16]{1,0:T(8,128)}, f32[1,16]{1,0:T(1,128)}) custom-call(f32[16,16]{1,0:T(8,128)} %get-tuple-element.6.token_in, f32[1,16]{1,0:T(1,128)} %get-tuple-element.7.seq_in), custom_call_target="tpu_custom_call" | custom-call | tf_op jit(solution)/shard_map/hand_over/pallas_call | solution.py:809
